TPU v7x, 32 devices: a whole 2x2x4 slice. The times are simulated.
32 devices in a mesh: ctx: 8 (over z, core), head: 4 (over y, x).
Axes of the slice: x: 2, y: 2, z: 4, core: 2. Of those that a mesh axis runs over, the one named last changes fastest.
Arguments:
- queries: bfloat16 [1024, 8192], P('ctx', 'head'), parts along dimension 1, may hold values from -17 to 17
- keys: bfloat16 [1024, 512], P('ctx', 'head'), parts along dimension 1, may hold values from -17 to 17
- values: bfloat16 [1024, 512], P('ctx', 'head'), parts along dimension 1, may hold values from -6 to 6
- block_position: int32 [8], P('ctx'), may hold values from 0 to 7, each once
Outputs:
- attended: bfloat16 [1024, 8192], P('ctx', 'head'), parts along dimension 1
There are 4 independent parts, one for each index of `head`. A program takes and returns all parts, laid end to end along the dimension named above; an argument that names none is the same for every part. Nothing has to cross between parts.
All inputs are finite; a program needn't handle non-finite values.
Results may differ from a plain program's by a relative error of at most 0.005.
Values may be sent and summed in bfloat16 or wider, within the bound.
No kernel may reach another device: no remote copies, remote signals or barrier semaphores. Data moves between devices by JAX's collectives and lax.ppermute only.
A program may use at most 128 MiB of HBM per device.

v0:
```python
import math

import jax
import jax.numpy as jnp
from jax import lax
from jax.sharding import PartitionSpec as P

HEAD_DIM = 128
QHEADS = 16
BLOCK = 128


def body(queries, keys, values, block_position):
    local_rows = queries.shape[0]
    places = lax.all_gather(block_position, "ctx", axis=0, tiled=True)
    myself = lax.axis_index("ctx")
    row_ids = myself * local_rows + jnp.arange(local_rows, dtype=jnp.int32)
    query_pos = jnp.take(places, row_ids // BLOCK) * BLOCK + row_ids % BLOCK
    latest = jnp.max(query_pos)
    query_heads = queries.reshape(local_rows, QHEADS, HEAD_DIM).transpose(1, 0, 2)
    scale = 1.0 / math.sqrt(HEAD_DIM)
    initial = (
        jnp.full((QHEADS, local_rows), -1e30, jnp.float32),
        jnp.zeros((QHEADS, local_rows), jnp.float32),
        jnp.zeros((QHEADS, local_rows, HEAD_DIM), jnp.float32),
    )
    key_piece = lax.all_gather(keys, "ctx", axis=0, tiled=True)
    value_piece = lax.all_gather(values, "ctx", axis=0, tiled=True)
    piece_rows = key_piece.shape[0]
    key_ids = jnp.arange(piece_rows, dtype=jnp.int32)
    key_pos = jnp.take(places, key_ids // BLOCK) * BLOCK + key_ids % BLOCK

    def attend(state_in):
        running_max, denominator, numerator = state_in
        scores = (
            jnp.einsum("htd,nd->htn", query_heads, key_piece, preferred_element_type=jnp.float32)
            * scale
        )
        visible = key_pos[None, None, :] <= query_pos[None, :, None]
        new_max = jnp.maximum(running_max, jnp.max(jnp.where(visible, scores, -1e30), axis=-1))
        weights = jnp.where(visible, jnp.exp(scores - new_max[..., None]), 0.0)
        denominator = jnp.sum(weights, axis=-1)
        numerator = jnp.einsum(
            "htn,nd->htd",
            weights.astype(jnp.bfloat16),
            value_piece,
            preferred_element_type=jnp.float32,
        )
        return (new_max, denominator, numerator)

    final = lax.cond(jnp.min(key_pos) > latest, lambda state_in: state_in, attend, initial)
    running_max, denominator, numerator = final
    output = (numerator / denominator[..., None]).astype(jnp.bfloat16)
    return output.transpose(1, 0, 2).reshape(local_rows, QHEADS * HEAD_DIM)


def solution(mesh):
    placed = (P("ctx", "head"), P("ctx", "head"), P("ctx", "head"), P("ctx"))
    return jax.shard_map(
        body, mesh=mesh, in_specs=placed, out_specs=P("ctx", "head"), check_vma=False
    )
```

profile of v0, /device:TPU:0, one launch (start us, length us, event | category | flops | bytes accessed | tf_op | source)
XLA Modules:
  0.0 63.8 jit_solution(7075929578409433718)
XLA Ops:
  0.7 1.2 %dynamic-slice = u32[1]{0:T(128)} dynamic-slice(u32[32]{0:T(128)} %constant.118, u32[]{:T(128)S(6)} %add.115), dynamic_slice_sizes={1} | dynamic-slice | bytes 12
  1.9 0.8 %dynamic-update-slice = s32[8]{0:T(128)S(1)} dynamic-update-slice(s32[8]{0:T(128)S(1)} %broadcast.303, s32[1]{0:T(128)S(6)} %copy.17, u32[]{:T(128)} %bitcast.2) | dynamic-update-slice | bytes 12
  2.7 10.6 %all-reduce = s32[8]{0:T(128)S(1)} all-reduce(s32[8]{0:T(128)S(1)} %dynamic-update-slice), channel_id=1, replica_groups=mesh['ctx'=8,'head'=4] {'ctx'}, use_global_device_ids=true, to_apply=%add | all-reduce | flops 8 | bytes 64
  13.3 0.7 %fusion.29 = (s32[1]{0:T(128)}, s32[1]{0:T(128)}, s32[1]{0:T(128)}, s32[1]{0:T(128)}, s32[1]{0:T(128)}, /*index=5*/s32[1]{0:T(128)}, s32[1]{0:T(128)}, s32[1]{0:T(128)}) fusion(s32[8]{0:T(128)S(1)} %all-reduce), kind=kLoop, calls=%fused_computation.69 | loop fusion | bytes 64 | tf_op jit(solution)/shard_map/jit(_take)/gather | solution.py:31
  14.0 5.7 %fusion.25 = (s32[]{:T(128)}, s32[128]{0:T(128)S(1)}) fusion(s32[]{:T(128)} %bitcast.10, s32[]{:T(128)} %bitcast.9, s32[]{:T(128)} %bitcast.8, s32[]{:T(128)} %bitcast.7, s32[]{:T(128)} %bitcast.6, s32[]{:T(128)} %bitcast.5, s32[]{:T(128)} %bitcast.4, s32[]{:T(128)} %bitcast.3, s32[]{:T(128)S(6)} %mul.15), kind=kLoop, calls=%fused_computation.67 | loop fusion | flops 8063 | bytes 552 | tf_op jit(solution)/shard_map/reduce_max | solution.py:19
  19.7 4.3 %compare_select_fusion.1 = s32[1024,1]{0,1:T(1,128)S(1)} fusion(s32[]{:T(128)} %bitcast.4, s32[]{:T(128)} %bitcast.5, s32[]{:T(128)} %bitcast.6, s32[]{:T(128)} %bitcast.7, s32[]{:T(128)} %bitcast.8, s32[]{:T(128)} %bitcast.10, s32[]{:T(128)} %bitcast.9), kind=kLoop, calls=%fused_computation.18 | loop fusion | flops 23552 | bytes 4124 | tf_op jit(solution)/shard_map/jit(_take)/gather | solution.py:31
  24.0 1.3 %fusion.27 = (s32[]{:T(128)}, s32[1024]{0:T(1024)S(1)}) fusion(pred[1024]{0:T(1024)(128)(4,1)S(1)} %compare_reduce_fusion, s32[1024]{0:T(1024)S(1)} %bitcast.45, s32[]{:T(128)} %bitcast.3), kind=kLoop, calls=%fused_computation.68 | loop fusion | flops 23551 | bytes 9224 | tf_op jit(solution)/shard_map/reduce_min | solution.py:51
  26.5 14.4 %all_gather.10 = bf16[1024,128]{1,0:T(8,128)(2,1)S(1)} all-gather(bf16[128,128]{1,0:T(8,128)(2,1)} %param.7), channel_id=1, replica_groups=mesh['ctx'=8,'head'=4] {'ctx'}, dimensions={0}, use_global_device_ids=true | all-gather | bytes 294912 | tf_op jit(solution)/shard_map/all_gather | solution.py:27
  40.9 14.4 %all_gather.11 = bf16[1024,128]{1,0:T(8,128)(2,1)S(1)} all-gather(bf16[128,128]{1,0:T(8,128)(2,1)} %param.8), channel_id=1, replica_groups=mesh['ctx'=8,'head'=4] {'ctx'}, dimensions={0}, use_global_device_ids=true | all-gather | bytes 294912 | tf_op jit(solution)/shard_map/all_gather | solution.py:28
  55.3 1.3 %copy.6 = bf16[128,2048]{0,1:T(8,128)(2,1)S(1)} copy(bf16[128,2048]{1,0:T(8,128)(2,1)} %param.6) | data formatting | bytes 1048576 | tf_op args[0]
  56.6 6.0 %conditional.1 = (f32[16,128]{1,0:T(8,128)S(1)}, f32[16,128,128]{2,1,0:T(8,128)S(1)}) conditional(s32[]{:T(128)} %convert_element_type.9, (s32[1024]{0:T(1024)S(1)}, s32[128]{0:T(128)S(1)}, bf16[16,128,128]{1,2,0:T(8,128)(2,1)S(1)}, bf16[1024,128]{1,0:T(8,128)(2,1)S(1)}, bf16[1024,128]{1,0:T(8,128)(2,1)S(1)}) %tuple.28, () %tuple.14), branch_computations={%region_2.5_spmd, %region_5.6_spmd} | conditional | flops 1096939520 | bytes 27841040 | solution.py:51
  56.6 0.1 broadcast_compare_fusion
  56.8 1.6 %select_reduce_fusion = (f32[16,128]{1,0:T(8,128)S(1)}, f32[16,128,1024]{2,1,0:T(8,128)S(1)}) fusion(pred[128,1024]{1,0:T(8,128)(4,1)S(1)} %broadcast_compare_fusion, bf16[16,128,128]{1,2,0:T(8,128)(2,1)S(1)} %get-tuple-element.26, bf16[1024,128]{1,0:T(8,128)(2,1)S(1)} %get-tuple-element.18), kind=kOutput, calls=%fused_computation.1 | convolution fusion | flops 543160320 | bytes 9314304 | tf_op jit(solution)/shard_map/cond/branch_0_fun/htd,nd->htn/dot_general | solution.py:36
  58.4 2.4 %fusion.1 = f32[16,128]{1,0:T(8,128)S(1)} fusion(f32[16,128,1024]{2,1,0:T(8,128)S(1)} %get-tuple-element.34, f32[16,128]{1,0:T(8,128)S(1)} %broadcast_maximum_fusion, pred[128,1024]{1,0:T(8,128)(4,1)S(1)} %broadcast_compare_fusion), kind=kLoop, calls=%fused_computation.3 | loop fusion | flops 8386560 | bytes 8536064 | tf_op jit(solution)/shard_map/cond/branch_0_fun/reduce_sum | solution.py:42
  60.8 1.8 %fusion.2 = f32[16,128,128]{2,1,0:T(8,128)S(1)} fusion(f32[16,128,1024]{2,1,0:T(8,128)S(1)} %get-tuple-element.34, f32[16,128]{1,0:T(8,128)S(1)} %broadcast_maximum_fusion, pred[128,1024]{1,0:T(8,128)(4,1)S(1)} %broadcast_compare_fusion, bf16[1024,128]{1,0:T(8,128)(2,1)S(1)} %get-tuple-element.19), kind=kOutput, calls=%fused_computation.4 | convolution fusion | flops 545259520 | bytes 9838592 | tf_op jit(solution)/shard_map/cond/branch_0_fun/htn,nd->htd/dot_general | solution.py:43
  62.7 1.1 %copy_bitcast_fusion = bf16[128,2048]{1,0:T(8,128)(2,1)} fusion(f32[16,128,128]{2,1,0:T(8,128)S(1)} %get-tuple-element.22, f32[16,128]{1,0:T(8,128)S(1)} %get-tuple-element.23), kind=kLoop, calls=%fused_computation.14 | loop fusion | flops 524288 | bytes 1581056 | tf_op jit(solution)/shard_map/reshape | solution.py:54
  (3 shorter events, 0.0 us)
where the time goes:
time: 64.2 us; the launch traced here: 63.8 us
  blocking collectives  39.4 us (61%)
  other arithmetic  15 us (23%)
  local copies, waits for them, and re-layouts  4 us (6%)
  matrix products  3.44 us (5%)
  between operations  1.94 us (3%)
    all_gather x1, blocking collectives, body(): key_piece = lax.all_gather(keys, 'ctx', axis=0, tiled=True)  14.4 us
    all_gather x1, blocking collectives, body(): value_piece = lax.all_gather(values, 'ctx', axis=0, tiled=True)  14.4 us
    unnamed x1, blocking collectives  10.6 us
    reduce_max x1, other arithmetic, body(): latest = jnp.max(query_pos)  5.67 us
    gather x2, other arithmetic, body(): key_pos = jnp.take(places, key_ids // BLOCK) * BLOCK + key_ids % BLOCK  4.32 us
    unnamed x4, local copies, waits for them, and re-layouts  3.31 us
    reduce_sum x1, other arithmetic, attend(): denominator = jnp.sum(weights, axis=-1)  2.41 us
    dot_general x1, matrix products, attend(): jnp.einsum('htn,nd->htd', weights.astype(jnp.bfloat16), value_piece, pref...  1.84 us

commit v1 on v0

v1 whole, which is shorter than its diff:
```python
import functools
import math

import jax
import jax.numpy as jnp
from jax import lax
from jax.experimental import pallas as pl
from jax.experimental.pallas import tpu as pltpu
from jax.sharding import PartitionSpec as P

HEAD_DIM = 128
QHEADS = 16
BLOCK = 128
CORES = 2
POS_ROWS = 16
PACKET = 2 * BLOCK + POS_ROWS
PAIR = 2 * BLOCK
LOG2E_SCALE = math.log2(math.e) / math.sqrt(HEAD_DIM)
ABT = (((1,), (1,)), ((), ()))


def pack(keys, values, block_position):
    tag = jnp.broadcast_to(block_position.astype(keys.dtype)[:, None], (POS_ROWS, HEAD_DIM))
    return jnp.concatenate([keys, values, tag], axis=0)


def attend_kernel(chunk, unroll, q_ref, mine_ref, other_ref, o_ref, k_all, vt_all, scores, peaks):
    pieces = mine_ref.shape[0] // PACKET
    packets = [(ref, i * PACKET) for ref in (mine_ref, other_ref) for i in range(pieces)]
    count = len(packets)
    total = count * BLOCK
    last = QHEADS // 2 - 1

    vt_all[HEAD_DIM:, :] = jnp.ones((POS_ROWS, total), vt_all.dtype)
    for i, (ref, base) in enumerate(packets):
        k_all[i * BLOCK : (i + 1) * BLOCK, :] = ref[base : base + BLOCK, :]
        vt_all[:HEAD_DIM, i * BLOCK : (i + 1) * BLOCK] = ref[base + BLOCK : base + 2 * BLOCK, :].T

    def place(i):
        ref, base = packets[i]
        tag = ref[base + 2 * BLOCK : base + PACKET, :].astype(jnp.float32)
        return jnp.concatenate([tag[:8], tag[:8]], axis=1)

    own = place(0)
    seen = [None] + [place(i) < own for i in range(1, count)]
    key = lax.broadcasted_iota(jnp.int32, (BLOCK, PAIR), 0)
    row = lax.broadcasted_iota(jnp.int32, (BLOCK, PAIR), 1) % BLOCK
    diagonal = key <= row

    def columns(head):
        if isinstance(head, int):
            return slice(head * HEAD_DIM, (head + 1) * HEAD_DIM)
        return pl.ds(pl.multiple_of(head * HEAD_DIM, HEAD_DIM), HEAD_DIM)

    def pair_queries(pair):
        return jnp.concatenate([q_ref[:, columns(2 * pair + j)] for j in range(2)], axis=0)

    def score(slot, start, q, peak):
        s = lax.dot_general(
            k_all[start : start + chunk, :], q, ABT, preferred_element_type=jnp.float32
        )
        for j in range(chunk // BLOCK):
            i = start // BLOCK + j
            block = s[j * BLOCK : (j + 1) * BLOCK]
            if i == 0:
                block = jnp.where(diagonal, block, -1e30)
            scores[slot, i * BLOCK : (i + 1) * BLOCK, :] = block
            top = block.reshape(BLOCK // 8, 8, PAIR).max(axis=0)
            if i > 0:
                top = jnp.where(seen[i], top, -1e30)
            peak = top if peak is None else jnp.maximum(peak, top)
        return peak

    def weigh(slot, start, peak, acc):
        weights = []
        for j in range(chunk // BLOCK):
            i = start // BLOCK + j
            bound = peak if i == 0 else jnp.where(seen[i], peak, 1e30)
            s = scores[slot, i * BLOCK : (i + 1) * BLOCK, :].reshape(BLOCK // 8, 8, PAIR)
            w = jnp.exp2((s - bound[None]) * LOG2E_SCALE)
            weights.append(w.reshape(BLOCK, PAIR).astype(jnp.bfloat16))
        part = jnp.dot(
            vt_all[:, start : start + chunk],
            jnp.concatenate(weights, axis=0),
            preferred_element_type=jnp.float32,
        )
        return part if acc is None else acc + part

    def keep(slot, peak):
        peaks[slot] = jnp.broadcast_to(peak.max(axis=0, keepdims=True), (8, PAIR))

    def write(pair, acc):
        out = (acc[:HEAD_DIM] / acc[HEAD_DIM : HEAD_DIM + 1]).astype(o_ref.dtype)
        for j in range(2):
            o_ref[:, columns(2 * pair + j)] = out[:, j * BLOCK : (j + 1) * BLOCK].T

    def step(pair, slot, ahead):
        q = pair_queries(pair + 1) if ahead else None
        bound = peaks[slot]
        peak = acc = None
        for start in range(0, total, chunk):
            if ahead:
                peak = score(1 - slot, start, q, peak)
            acc = weigh(slot, start, bound, acc)
        if ahead:
            keep(1 - slot, peak)
        write(pair, acc)

    q, peak = pair_queries(0), None
    for start in range(0, total, chunk):
        peak = score(0, start, q, peak)
    keep(0, peak)
    if unroll:
        for pair in range(last):
            step(pair, pair % 2, True)
    else:

        def two(i, carry):
            step(2 * i, 0, True)
            step(2 * i + 1, 1, True)
            return carry

        lax.fori_loop(0, last // 2, two, 0)
        step(last - 1, 0, True)
    step(last, last % 2, False)


def attend(queries, mine, other):
    total = 2 * (mine.shape[0] // PACKET) * BLOCK
    chunk = math.gcd(total, 8 * BLOCK)
    vmem = pl.BlockSpec(memory_space=pltpu.VMEM)
    return pl.pallas_call(
        functools.partial(attend_kernel, chunk, total == chunk),
        out_shape=jax.ShapeDtypeStruct(queries.shape, queries.dtype),
        in_specs=[vmem] * 3,
        out_specs=vmem,
        scratch_shapes=[
            pltpu.VMEM((total, HEAD_DIM), jnp.bfloat16),
            pltpu.VMEM((HEAD_DIM + POS_ROWS, total), jnp.bfloat16),
            pltpu.VMEM((2, total, PAIR), jnp.float32),
            pltpu.VMEM((2, 8, PAIR), jnp.float32),
        ],
        compiler_params=pltpu.CompilerParams(vmem_limit_bytes=24 * 2**20),
    )(queries, mine, other)


def body(size, queries, keys, values, block_position):
    packet = pack(keys, values, block_position)
    gathered = [packet]
    for shift in range(CORES, size, CORES):
        pairs = [(i, (i + shift) % size) for i in range(size)]
        gathered.append(lax.ppermute(packet, "ctx", pairs))
    mine = jnp.concatenate(gathered, axis=0)
    other = lax.ppermute(mine, "ctx", [(i, i ^ 1) for i in range(size)])
    return attend(queries, mine, other)


def solution(mesh):
    placed = (P("ctx", "head"), P("ctx", "head"), P("ctx", "head"), P("ctx"))
    return jax.shard_map(
        functools.partial(body, mesh.shape["ctx"]),
        mesh=mesh,
        in_specs=placed,
        out_specs=P("ctx", "head"),
        check_vma=False,
    )
```

time: 64.2 us -> 18.9 us (0.29)
  blocking collectives: 39.4 us -> 0 us
  other arithmetic: 15 us -> 0.78 us
  starting transfers between devices: 0 us -> 6.16 us
  waiting for transfers between devices: 0 us -> 5.76 us
  Pallas kernels: 0 us -> 3.53 us
  matrix products: 3.44 us -> 0 us
  local copies, waits for them, and re-layouts: 4 us -> 1.58 us
  between operations: 1.94 us -> 0.75 us
    all_gather x2 -> x0, blocking collectives: 28.8 us -> none  [the longest x1 14.4 us: body(): key_piece = lax.all_gather(keys, 'ctx', axis=0, tiled=True)]
    unnamed x1 -> x0, blocking collectives: 10.6 us -> none
    ppermute x0 -> x4, starting transfers between devices: none -> 6.16 us  [the longest x3 6.09 us: body(): gathered.append(lax.ppermute(packet, 'ctx', pairs))]
    ppermute x0 -> x4, waiting for transfers between devices: none -> 5.76 us  [the longest x3 4.22 us: body(): gathered.append(lax.ppermute(packet, 'ctx', pairs))]
    reduce_max x1 -> x0, other arithmetic: 5.67 us -> none  [body(): latest = jnp.max(query_pos)]
    gather x2 -> x0, other arithmetic: 4.32 us -> none  [body(): key_pos = jnp.take(places, key_ids // BLOCK) * BLOCK + key_ids % BLOCK]
    pallas_call x0 -> x1, Pallas kernels: none -> 3.53 us  [attend(): pl.pallas_call(functools.partial(attend_kernel, chunk, total == chunk), o...]
    dot_general x2 -> x0, matrix products: 3.44 us -> none  [the longest x1 1.84 us: attend(): jnp.einsum('htn,nd->htd', weights.astype(jnp.bfloat16), value_piece, pref...]
  transfers between devices with their start and end apart: 0 -> 4, of which waited for: 0 -> 3; matrix products, arithmetic and copies ran while one was open for 0% -> 8% of each run, Pallas kernels for 0% -> 0%
where the time goes in v1:
time: 18.9 us; the launch traced here: 18.6 us
  starting transfers between devices  6.16 us (33%)
  waiting for transfers between devices  5.76 us (30%)
  Pallas kernels  3.53 us (19%)
  local copies, waits for them, and re-layouts  1.58 us (8%)
  other arithmetic  0.78 us (4%)
  between operations  0.75 us (4%)
    ppermute x3, starting transfers between devices, body(): gathered.append(lax.ppermute(packet, 'ctx', pairs))  6.09 us
    ppermute x3, waiting for transfers between devices, body(): gathered.append(lax.ppermute(packet, 'ctx', pairs))  4.22 us
    pallas_call x1, Pallas kernels, attend(): pl.pallas_call(functools.partial(attend_kernel, chunk, total == chunk), o...  3.53 us
    unnamed x7, local copies, waits for them, and re-layouts  1.56 us
    ppermute x1, waiting for transfers between devices, body(): other = lax.ppermute(mine, 'ctx', [(i, i ^ 1) for i in range(size)])  1.55 us
    concatenate x1, other arithmetic, pack(): return jnp.concatenate([keys, values, tag], axis=0)  0.78 us
  transfers between devices with their start and end apart: 4, of which 3 were waited for; matrix products, arithmetic and copies ran while one was open for 8% of the time, Pallas kernels for 0%

profile of v1, /device:TPU:0, one launch (start us, length us, event | category | flops | bytes accessed | tf_op | source)
XLA Modules:
  0.0 18.6 jit_solution(5166383349716594616)
XLA Ops:
  0.0 0.0 copy-start
  0.7 0.8 %pad_maximum_fusion = bf16[272,128]{1,0:T(8,128)(2,1)S(1)} fusion(bf16[16,128]{1,0:T(8,128)(2,1)S(1)} %broadcast_in_dim.9, bf16[128,128]{1,0:T(8,128)(2,1)} %param.6, bf16[128,128]{1,0:T(8,128)(2,1)} %param.5), kind=kLoop, calls=%fused_computation | loop fusion | flops 208896 | bytes 139264 | tf_op jit(solution)/shard_map/concatenate | solution.py:24
  1.5 5.1 %collective-permute-start.2 = (bf16[272,128]{1,0:T(8,128)(2,1)S(1)}, bf16[272,128]{1,0:T(8,128)(2,1)S(1)}, u32[]{:S(2)}, u32[]{:S(2)}) collective-permute-start(bf16[272,128]{1,0:T(8,128)(2,1)S(1)} %pad_maximum_fusion), channel_id=1, source_target_pairs={{0,24},{4,28},{8,0},{12,4},{16,8},{20,12},{24,16},{28,20},{1,25},{... | collective-permute-start | bytes 208904 | tf_op jit(solution)/shard_map/ppermute | solution.py:152
  6.6 0.0 collective-permute-start.1
  6.6 1.0 %collective-permute-start = (bf16[272,128]{1,0:T(8,128)(2,1)S(1)}, bf16[272,128]{1,0:T(8,128)(2,1)S(1)}, u32[]{:S(2)}, u32[]{:S(2)}) collective-permute-start(bf16[272,128]{1,0:T(8,128)(2,1)S(1)} %pad_maximum_fusion), channel_id=1, source_target_pairs={{0,8},{4,12},{8,16},{12,20},{16,24},{20,28},{24,0},{28,4},{1,9},{5... | collective-permute-start | bytes 208904 | tf_op jit(solution)/shard_map/ppermute | solution.py:152
  7.6 0.8 %constant_dynamic-update-slice_fusion.5 = bf16[1088,128]{1,0:T(8,128)(2,1)S(1)} fusion(bf16[128,128]{1,0:T(8,128)(2,1)} %param.5), kind=kLoop, calls=%fused_computation.6 | loop fusion | bytes 65536
  8.4 0.8 %constant_dynamic-update-slice_fusion.4 = bf16[1088,128]{1,0:T(8,128)(2,1)S(1)} fusion(bf16[1088,128]{1,0:T(8,128)(2,1)S(1)} %constant_dynamic-update-slice_fusion.5, bf16[128,128]{1,0:T(8,128)(2,1)} %param.6), kind=kLoop, calls=%fused_computation.5 | loop fusion | bytes 65536
  9.1 3.7 %collective-permute-done = bf16[272,128]{1,0:T(8,128)(2,1)S(1)} collective-permute-done((bf16[272,128]{1,0:T(8,128)(2,1)S(1)}, bf16[272,128]{1,0:T(8,128)(2,1)S(1)}, u32[]{:S(2)}, u32[]{:S(2)}) %collective-permute-start) | collective-permute-done | bytes 69664 | tf_op jit(solution)/shard_map/ppermute | solution.py:152
  12.8 0.6 %collective-permute-done.1 = bf16[272,128]{1,0:T(8,128)(2,1)S(1)} collective-permute-done((bf16[272,128]{1,0:T(8,128)(2,1)S(1)}, bf16[272,128]{1,0:T(8,128)(2,1)S(1)}, u32[]{:S(2)}, u32[]{:S(2)}) %collective-permute-start.1) | collective-permute-done | bytes 69664 | tf_op jit(solution)/shard_map/ppermute | solution.py:152
  13.4 0.0 collective-permute-done.2
  13.4 0.1 collective-permute-start.3
  13.5 1.5 %collective-permute-done.3.other_ref = bf16[1088,128]{1,0:T(8,128)(2,1)S(1)} collective-permute-done((bf16[1088,128]{1,0:T(8,128)(2,1)S(1)}, bf16[1088,128]{1,0:T(8,128)(2,1)S(1)}, u32[]{:S(2)}, u32[]{:S(2)}) %collective-permute-start.3) | collective-permute-done | bytes 278560 | tf_op jit(solution)/shard_map/ppermute | solution.py:154
  15.0 0.0 copy-done
  15.0 3.5 %shard_map.46 = bf16[128,2048]{1,0:T(8,128)(2,1)} custom-call(bf16[128,2048]{1,0:T(8,128)(2,1)S(1)} %copy-done, bf16[1088,128]{1,0:T(8,128)(2,1)S(1)} %constant_dynamic-update-slice_fusion.mine_ref, bf16[1088,128]{1,0:T(8,128)(2,1)S(1)} %collective-permute-done.3.other_ref), custom_call_target="tpu_custom_call" | custom-call | tf_op jit(solution)/shard_map/pallas_call | solution.py:132
  (5 shorter events, 0.1 us)
Async XLA Ops:
  0.0 15.0 %copy-start = (bf16[128,2048]{1,0:T(8,128)(2,1)S(1)}, bf16[128,2048]{1,0:T(8,128)(2,1)}, u32[]{:S(2)}) copy-start(bf16[128,2048]{1,0:T(8,128)(2,1)} %q_ref.1) | copy-start | bytes 1572868
  1.5 11.9 %collective-permute-start.2 = (bf16[272,128]{1,0:T(8,128)(2,1)S(1)}, bf16[272,128]{1,0:T(8,128)(2,1)S(1)}, u32[]{:S(2)}, u32[]{:S(2)}) collective-permute-start(bf16[272,128]{1,0:T(8,128)(2,1)S(1)} %pad_maximum_fusion), channel_id=1, source_target_pairs={{0,24},{4,28},{8,0},{12,4},{16,8},{20,12},{24,16},{28,20},{1,25},{... | collective-permute-start | bytes 208904 | tf_op jit(solution)/shard_map/ppermute | solution.py:152
  6.6 6.8 %collective-permute-start.1 = (bf16[272,128]{1,0:T(8,128)(2,1)S(1)}, bf16[272,128]{1,0:T(8,128)(2,1)S(1)}, u32[]{:S(2)}, u32[]{:S(2)}) collective-permute-start(bf16[272,128]{1,0:T(8,128)(2,1)S(1)} %pad_maximum_fusion), channel_id=1, source_target_pairs={{0,16},{4,20},{8,24},{12,28},{16,0},{20,4},{24,8},{28,12},{1,17},{... | collective-permute-start | bytes 208904 | tf_op jit(solution)/shard_map/ppermute | solution.py:152
  6.6 6.2 %collective-permute-start = (bf16[272,128]{1,0:T(8,128)(2,1)S(1)}, bf16[272,128]{1,0:T(8,128)(2,1)S(1)}, u32[]{:S(2)}, u32[]{:S(2)}) collective-permute-start(bf16[272,128]{1,0:T(8,128)(2,1)S(1)} %pad_maximum_fusion), channel_id=1, source_target_pairs={{0,8},{4,12},{8,16},{12,20},{16,24},{20,28},{24,0},{28,4},{1,9},{5... | collective-permute-start | bytes 208904 | tf_op jit(solution)/shard_map/ppermute | solution.py:152
  13.4 1.6 %collective-permute-start.3 = (bf16[1088,128]{1,0:T(8,128)(2,1)S(1)}, bf16[1088,128]{1,0:T(8,128)(2,1)S(1)}, u32[]{:S(2)}, u32[]{:S(2)}) collective-permute-start(bf16[1088,128]{1,0:T(8,128)(2,1)S(1)} %constant_dynamic-update-slice_fusion.mine_ref), channel_id=1, source_target_pairs={{0,4},{4,0},{8,12},{12,8},{16,20},{20,16},{24,28},{28,24},{1,5},{5... | collective-permute-start | bytes 835592 | tf_op jit(solution)/shard_map/ppermute | solution.py:154

commit v2 on v1

v2 whole, which is shorter than its diff:
```python
import functools
import math

import jax
import jax.numpy as jnp
from jax import lax
from jax.experimental import pallas as pl
from jax.experimental.pallas import tpu as pltpu
from jax.sharding import PartitionSpec as P


HEAD_DIM = 128
QHEADS = 16
BLOCK = 128
CORES = 2
POS_ROWS = 16
PACKET = 2 * BLOCK + POS_ROWS
PAIR = 2 * BLOCK
LOG2E_SCALE = math.log2(math.e) / math.sqrt(HEAD_DIM)
ABT = (((1,), (1,)), ((), ()))


def pack(keys, values, block_position):
    tag = jnp.broadcast_to(block_position.astype(keys.dtype)[:, None], (POS_ROWS, HEAD_DIM))
    return jnp.concatenate([keys, values, tag], axis=0)


def stage_kernel(source, target, sem):
    copy = pltpu.make_async_copy(source, target, sem)
    copy.start()
    copy.wait()


def stage(queries):
    return pl.pallas_call(
        stage_kernel,
        out_shape=pltpu.VMEM(queries.shape, queries.dtype),
        in_specs=[pl.BlockSpec(memory_space=pltpu.HBM)],
        out_specs=pl.BlockSpec(memory_space=pltpu.VMEM),
        scratch_shapes=[pltpu.SemaphoreType.DMA],
        compiler_params=pltpu.CompilerParams(vmem_limit_bytes=2**20),
    )(pltpu.with_memory_space_constraint(queries, pltpu.HBM))


def attend_kernel(chunk, unroll, first, final, *refs):
    q_ref, mine_ref, *refs = refs
    keys_ref = mine_ref
    if not first:
        keys_ref, old_acc, old_peak, *refs = refs
    outs, (k_all, vt_all, scores, peaks) = refs[:-4], refs[-4:]
    count = keys_ref.shape[0] // PACKET
    total = count * BLOCK
    last = QHEADS // 2 - 1

    def place(ref, i):
        tag = ref[i * PACKET + 2 * BLOCK : (i + 1) * PACKET, :].astype(jnp.float32)
        return jnp.concatenate([tag[:8], tag[:8]], axis=1)

    vt_all[HEAD_DIM:, :] = jnp.ones((POS_ROWS, total), vt_all.dtype)
    for i in range(count):
        base = i * PACKET
        rows = slice(i * BLOCK, (i + 1) * BLOCK)
        k_all[rows, :] = keys_ref[base : base + BLOCK, :]
        vt_all[:HEAD_DIM, rows] = keys_ref[base + BLOCK : base + 2 * BLOCK, :].T

    own = place(mine_ref, 0)
    seen = [None if first and i == 0 else place(keys_ref, i) < own for i in range(count)]
    key = lax.broadcasted_iota(jnp.int32, (BLOCK, PAIR), 0)
    row = lax.broadcasted_iota(jnp.int32, (BLOCK, PAIR), 1) % BLOCK
    diagonal = key <= row

    def columns(head):
        if isinstance(head, int):
            return slice(head * HEAD_DIM, (head + 1) * HEAD_DIM)
        return pl.ds(pl.multiple_of(head * HEAD_DIM, HEAD_DIM), HEAD_DIM)

    def pair_queries(pair):
        return jnp.concatenate([q_ref[:, columns(2 * pair + j)] for j in range(2)], axis=0)

    def score(slot, start, q, peak):
        s = lax.dot_general(
            k_all[start : start + chunk, :], q, ABT, preferred_element_type=jnp.float32
        )
        for j in range(chunk // BLOCK):
            i = start // BLOCK + j
            block = s[j * BLOCK : (j + 1) * BLOCK]
            if seen[i] is None:
                block = jnp.where(diagonal, block, -1e30)
            scores[slot, i * BLOCK : (i + 1) * BLOCK, :] = block
            top = block.reshape(BLOCK // 8, 8, PAIR).max(axis=0)
            if seen[i] is not None:
                top = jnp.where(seen[i], top, -1e30)
            peak = top if peak is None else jnp.maximum(peak, top)
        return peak

    def weigh(slot, start, peak, acc):
        weights = []
        for j in range(chunk // BLOCK):
            i = start // BLOCK + j
            bound = peak if seen[i] is None else jnp.where(seen[i], peak, 1e30)
            s = scores[slot, i * BLOCK : (i + 1) * BLOCK, :].reshape(BLOCK // 8, 8, PAIR)
            w = jnp.exp2((s - bound[None]) * LOG2E_SCALE)
            weights.append(w.reshape(BLOCK, PAIR).astype(jnp.bfloat16))
        part = jnp.dot(
            vt_all[:, start : start + chunk],
            jnp.concatenate(weights, axis=0),
            preferred_element_type=jnp.float32,
        )
        return part if acc is None else acc + part

    def keep(pair, slot, peak):
        peak = jnp.broadcast_to(peak.max(axis=0, keepdims=True), (8, PAIR))
        if not first:
            peak = jnp.maximum(peak, old_peak[pair])
        if not final:
            outs[1][pair] = peak
        peaks[slot] = peak

    def write(pair, acc, peak):
        if not first:
            alpha = jnp.exp2((old_peak[pair] - peak) * LOG2E_SCALE)
            old = old_acc[pair].reshape(-1, 8, PAIR) * alpha[None]
            acc = acc + old.reshape(acc.shape)
        if not final:
            outs[0][pair] = acc
            return
        out = (acc[:HEAD_DIM] / acc[HEAD_DIM : HEAD_DIM + 1]).astype(outs[0].dtype)
        for j in range(2):
            outs[0][:, columns(2 * pair + j)] = out[:, j * BLOCK : (j + 1) * BLOCK].T

    def step(pair, slot, ahead):
        q = pair_queries(pair + 1) if ahead else None
        bound = peaks[slot]
        peak = acc = None
        for start in range(0, total, chunk):
            if ahead:
                peak = score(1 - slot, start, q, peak)
            acc = weigh(slot, start, bound, acc)
        if ahead:
            keep(pair + 1, 1 - slot, peak)
        write(pair, acc, bound)

    q, peak = pair_queries(0), None
    for start in range(0, total, chunk):
        peak = score(0, start, q, peak)
    keep(0, 0, peak)
    if unroll:
        for pair in range(last):
            step(pair, pair % 2, True)
    else:

        def two(i, carry):
            step(2 * i, 0, True)
            step(2 * i + 1, 1, True)
            return carry

        lax.fori_loop(0, last // 2, two, 0)
        step(last - 1, 0, True)
    step(last, last % 2, False)


def attend(queries, mine, state, keys, final):
    total = keys.shape[0] // PACKET * BLOCK
    chunk = math.gcd(total, 4 * BLOCK)
    vmem = pl.BlockSpec(memory_space=pltpu.VMEM)
    args = (queries, mine) if state is None else (queries, mine, keys, *state)
    shapes = (
        jax.ShapeDtypeStruct((QHEADS // 2, HEAD_DIM + POS_ROWS, PAIR), jnp.float32),
        jax.ShapeDtypeStruct((QHEADS // 2, 8, PAIR), jnp.float32),
    )
    return pl.pallas_call(
        functools.partial(attend_kernel, chunk, total == chunk, state is None, final),
        out_shape=jax.ShapeDtypeStruct(queries.shape, queries.dtype) if final else shapes,
        in_specs=[vmem] * len(args),
        out_specs=vmem if final else (vmem, vmem),
        scratch_shapes=[
            pltpu.VMEM((total, HEAD_DIM), jnp.bfloat16),
            pltpu.VMEM((HEAD_DIM + POS_ROWS, total), jnp.bfloat16),
            pltpu.VMEM((2, total, PAIR), jnp.float32),
            pltpu.VMEM((2, 8, PAIR), jnp.float32),
        ],
        compiler_params=pltpu.CompilerParams(vmem_limit_bytes=24 * 2**20),
    )(*args)


def body(size, queries, keys, values, block_position):
    packet = lax.optimization_barrier(pack(keys, values, block_position))
    arrived = []
    for shift in range(size - CORES, 0, -CORES):
        pairs = [(i, (i + shift) % size) for i in range(size)]
        arrived.append(lax.ppermute(packet, "ctx", pairs))
    queries = stage(queries)
    arrived.append(packet)
    arrived.reverse()
    half = len(arrived) // 2
    state = mine = None
    for name, group in (("near", arrived[:half]), ("far", arrived[half:])):
        group = jnp.concatenate(group, axis=0)
        mine = group if mine is None else mine
        partner = lax.ppermute(group, "ctx", [(i, i ^ 1) for i in range(size)])
        state = attend(queries, mine, state, group, False)
        state = attend(queries, mine, state, partner, name == "far")
    return state


def solution(mesh):
    placed = (P("ctx", "head"), P("ctx", "head"), P("ctx", "head"), P("ctx"))
    return jax.shard_map(
        functools.partial(body, mesh.shape["ctx"]),
        mesh=mesh,
        in_specs=placed,
        out_specs=P("ctx", "head"),
        check_vma=False,
    )
```

time: 18.9 us -> 19 us (level)
  Pallas kernels: 3.53 us -> 6.41 us
  waiting for transfers between devices: 5.76 us -> 3.5 us
  local copies, waits for them, and re-layouts: 1.58 us -> 0.03 us
  starting transfers between devices: 6.16 us -> 7.18 us
    pallas_call x1 -> x5, Pallas kernels: 3.53 us -> 6.41 us  [the longest x4 5.36 us: attend(): pl.pallas_call(functools.partial(attend_kernel, chunk, total == chunk, st...]
    ppermute x4 -> x5, waiting for transfers between devices: 5.76 us -> 3.5 us  [the longest x3 3.5 us: body(): arrived.append(lax.ppermute(packet, 'ctx', pairs))]
    unnamed x7 -> x1, local copies, waits for them, and re-layouts: 1.56 us -> 0.01 us
    ppermute x4 -> x5, starting transfers between devices: 6.16 us -> 7.18 us  [the longest x3 7.04 us: body(): arrived.append(lax.ppermute(packet, 'ctx', pairs))]
  transfers between devices with their start and end apart: 4 -> 5, of which waited for: 3 -> 3; matrix products, arithmetic and copies ran while one was open for 8% -> 0% of each run, Pallas kernels for 0% -> 24%
where the time goes in v2:
time: 19 us; the launch traced here: 18.8 us
  starting transfers between devices  7.18 us (38%)
  Pallas kernels  6.41 us (34%)
  waiting for transfers between devices  3.5 us (18%)
  other arithmetic  0.89 us (5%)
  between operations  0.74 us (4%)
    ppermute x3, starting transfers between devices, body(): arrived.append(lax.ppermute(packet, 'ctx', pairs))  7.04 us
    pallas_call x4, Pallas kernels, attend(): pl.pallas_call(functools.partial(attend_kernel, chunk, total == chunk, st...  5.36 us
    ppermute x3, waiting for transfers between devices, body(): arrived.append(lax.ppermute(packet, 'ctx', pairs))  3.5 us
    pallas_call x1, Pallas kernels, stage(): pl.pallas_call(stage_kernel, out_shape=pltpu.VMEM(queries.shape, queries....  1.05 us
    concatenate x1, other arithmetic, pack(): return jnp.concatenate([keys, values, tag], axis=0)  0.88 us
  transfers between devices with their start and end apart: 5, of which 3 were waited for; matrix products, arithmetic and copies ran while one was open for 0% of the time, Pallas kernels for 24%

profile of v2, /device:TPU:0, one launch (start us, length us, event | category | flops | bytes accessed | tf_op | source)
XLA Modules:
  0.0 18.8 jit_solution(13983900931481491782)
XLA Ops:
  0.7 0.9 %maximum_maximum_fusion = bf16[272,128]{1,0:T(8,128)(2,1)S(1)} fusion(bf16[128,128]{1,0:T(8,128)(2,1)} %param.6, bf16[128,128]{1,0:T(8,128)(2,1)} %param.5, bf16[272]{0:T(512)(128)(2,1)S(1)} %pad.4.clone), kind=kLoop, calls=%fused_computation.1 | loop fusion | flops 208896 | bytes 135712 | tf_op jit(solution)/shard_map/concatenate | solution.py:25
  1.6 3.1 %collective-permute-start = (bf16[272,128]{1,0:T(8,128)(2,1)S(1)}, bf16[272,128]{1,0:T(8,128)(2,1)S(1)}, u32[]{:S(2)}, u32[]{:S(2)}) collective-permute-start(bf16[272,128]{1,0:T(8,128)(2,1)S(1)} %maximum_maximum_fusion), channel_id=1, source_target_pairs={{0,8},{4,12},{8,16},{12,20},{16,24},{20,28},{24,0},{28,4},{1,9},{5... | collective-permute-start | bytes 208904 | tf_op jit(solution)/shard_map/ppermute | solution.py:191
  4.7 2.6 %collective-permute-start.1 = (bf16[272,128]{1,0:T(8,128)(2,1)S(1)}, bf16[272,128]{1,0:T(8,128)(2,1)S(1)}, u32[]{:S(2)}, u32[]{:S(2)}) collective-permute-start(bf16[272,128]{1,0:T(8,128)(2,1)S(1)} %maximum_maximum_fusion), channel_id=1, source_target_pairs={{0,16},{4,20},{8,24},{12,28},{16,0},{20,4},{24,8},{28,12},{1,17},{... | collective-permute-start | bytes 208904 | tf_op jit(solution)/shard_map/ppermute | solution.py:191
  7.3 1.3 %collective-permute-start.2 = (bf16[272,128]{1,0:T(8,128)(2,1)S(1)}, bf16[272,128]{1,0:T(8,128)(2,1)S(1)}, u32[]{:S(2)}, u32[]{:S(2)}) collective-permute-start(bf16[272,128]{1,0:T(8,128)(2,1)S(1)} %maximum_maximum_fusion), channel_id=1, source_target_pairs={{0,24},{4,28},{8,0},{12,4},{16,8},{20,12},{24,16},{28,20},{1,25},{... | collective-permute-start | bytes 208904 | tf_op jit(solution)/shard_map/ppermute | solution.py:191
  8.6 0.6 %collective-permute-done = bf16[272,128]{1,0:T(8,128)(2,1)S(1)} collective-permute-done((bf16[272,128]{1,0:T(8,128)(2,1)S(1)}, bf16[272,128]{1,0:T(8,128)(2,1)S(1)}, u32[]{:S(2)}, u32[]{:S(2)}) %collective-permute-start) | collective-permute-done | bytes 69664 | tf_op jit(solution)/shard_map/ppermute | solution.py:191
  9.3 0.1 collective-permute-start.4
  9.3 2.6 %collective-permute-done.1 = bf16[272,128]{1,0:T(8,128)(2,1)S(1)} collective-permute-done((bf16[272,128]{1,0:T(8,128)(2,1)S(1)}, bf16[272,128]{1,0:T(8,128)(2,1)S(1)}, u32[]{:S(2)}, u32[]{:S(2)}) %collective-permute-start.1) | collective-permute-done | bytes 69664 | tf_op jit(solution)/shard_map/ppermute | solution.py:191
  12.0 0.2 %collective-permute-done.2 = bf16[272,128]{1,0:T(8,128)(2,1)S(1)} collective-permute-done((bf16[272,128]{1,0:T(8,128)(2,1)S(1)}, bf16[272,128]{1,0:T(8,128)(2,1)S(1)}, u32[]{:S(2)}, u32[]{:S(2)}) %collective-permute-start.2) | collective-permute-done | bytes 69664 | tf_op jit(solution)/shard_map/ppermute | solution.py:191
  12.2 0.1 collective-permute-start.3
  12.3 1.1 %shard_map.46.refs_0_ = bf16[128,2048]{1,0:T(8,128)(2,1)S(1)} custom-call(bf16[128,2048]{1,0:T(8,128)(2,1)} %source.1), custom_call_target="tpu_custom_call" | custom-call | tf_op jit(solution)/shard_map/pallas_call | solution.py:35
  13.4 1.1 %shard_map.47 = (f32[8,144,256]{2,1,0:T(8,128)S(1)}, f32[8,8,256]{2,1,0:T(8,128)S(1)}) custom-call(bf16[128,2048]{1,0:T(8,128)(2,1)S(1)} %shard_map.46.refs_0_, bf16[544,128]{1,0:T(8,128)(2,1)S(1)} %pad_maximum_fusion.refs_1_), custom_call_target="tpu_custom_call" | custom-call | tf_op jit(solution)/shard_map/pallas_call | solution.py:171
  14.5 0.0 collective-permute-done.4.refs_2_
  14.5 1.1 %shard_map.48 = (f32[8,144,256]{2,1,0:T(8,128)S(1)}, f32[8,8,256]{2,1,0:T(8,128)S(1)}) custom-call(bf16[128,2048]{1,0:T(8,128)(2,1)S(1)} %shard_map.46.refs_0_, bf16[544,128]{1,0:T(8,128)(2,1)S(1)} %pad_maximum_fusion.refs_1_, bf16[544,128]{1,0:T(8,128)(2,1)S(1)} %collective-permute-done.4.refs_2_, f32[8,144,256]{2,1,0:T(8,128)S(1)} %get-tuple-element.11.refs_3_, ...), custom_call_target="tpu_custom_call" | custom-call | tf_op jit(solution)/shard_map/pallas_call | solution.py:171
  15.6 1.1 %shard_map.49 = (f32[8,144,256]{2,1,0:T(8,128)S(1)}, f32[8,8,256]{2,1,0:T(8,128)S(1)}) custom-call(bf16[128,2048]{1,0:T(8,128)(2,1)S(1)} %shard_map.46.refs_0_, bf16[544,128]{1,0:T(8,128)(2,1)S(1)} %pad_maximum_fusion.refs_1_, bf16[544,128]{1,0:T(8,128)(2,1)S(1)} %constant_dynamic-update-slice_fusion.refs_2_, f32[8,144,256]{2,1,0:T(8,128)S(1)} %get-tuple-element.13.refs_3_, ...), custom_call_target="tpu_custom_call" | custom-call | tf_op jit(solution)/shard_map/pallas_call | solution.py:171
  16.8 0.0 collective-permute-done.3.refs_2_
  16.8 2.0 %shard_map.50 = bf16[128,2048]{1,0:T(8,128)(2,1)} custom-call(bf16[128,2048]{1,0:T(8,128)(2,1)S(1)} %shard_map.46.refs_0_, bf16[544,128]{1,0:T(8,128)(2,1)S(1)} %pad_maximum_fusion.refs_1_, bf16[544,128]{1,0:T(8,128)(2,1)S(1)} %collective-permute-done.3.refs_2_, f32[8,144,256]{2,1,0:T(8,128)S(1)} %get-tuple-element.15.refs_3_, ...), custom_call_target="tpu_custom_call" | custom-call | tf_op jit(solution)/shard_map/pallas_call | solution.py:171
  (5 shorter events, 0.0 us)
Async XLA Ops:
  1.6 7.7 %collective-permute-start = (bf16[272,128]{1,0:T(8,128)(2,1)S(1)}, bf16[272,128]{1,0:T(8,128)(2,1)S(1)}, u32[]{:S(2)}, u32[]{:S(2)}) collective-permute-start(bf16[272,128]{1,0:T(8,128)(2,1)S(1)} %maximum_maximum_fusion), channel_id=1, source_target_pairs={{0,8},{4,12},{8,16},{12,20},{16,24},{20,28},{24,0},{28,4},{1,9},{5... | collective-permute-start | bytes 208904 | tf_op jit(solution)/shard_map/ppermute | solution.py:191
  4.7 7.3 %collective-permute-start.1 = (bf16[272,128]{1,0:T(8,128)(2,1)S(1)}, bf16[272,128]{1,0:T(8,128)(2,1)S(1)}, u32[]{:S(2)}, u32[]{:S(2)}) collective-permute-start(bf16[272,128]{1,0:T(8,128)(2,1)S(1)} %maximum_maximum_fusion), channel_id=1, source_target_pairs={{0,16},{4,20},{8,24},{12,28},{16,0},{20,4},{24,8},{28,12},{1,17},{... | collective-permute-start | bytes 208904 | tf_op jit(solution)/shard_map/ppermute | solution.py:191
  7.3 4.9 %collective-permute-start.2 = (bf16[272,128]{1,0:T(8,128)(2,1)S(1)}, bf16[272,128]{1,0:T(8,128)(2,1)S(1)}, u32[]{:S(2)}, u32[]{:S(2)}) collective-permute-start(bf16[272,128]{1,0:T(8,128)(2,1)S(1)} %maximum_maximum_fusion), channel_id=1, source_target_pairs={{0,24},{4,28},{8,0},{12,4},{16,8},{20,12},{24,16},{28,20},{1,25},{... | collective-permute-start | bytes 208904 | tf_op jit(solution)/shard_map/ppermute | solution.py:191
  9.3 5.2 %collective-permute-start.4 = (bf16[544,128]{1,0:T(8,128)(2,1)S(1)}, bf16[544,128]{1,0:T(8,128)(2,1)S(1)}, u32[]{:S(2)}, u32[]{:S(2)}) collective-permute-start(bf16[544,128]{1,0:T(8,128)(2,1)S(1)} %pad_maximum_fusion.refs_1_), channel_id=1, source_target_pairs={{0,4},{4,0},{8,12},{12,8},{16,20},{20,16},{24,28},{28,24},{1,5},{5... | collective-permute-start | bytes 417800 | tf_op jit(solution)/shard_map/ppermute | solution.py:200
  12.2 4.5 %collective-permute-start.3 = (bf16[544,128]{1,0:T(8,128)(2,1)S(1)}, bf16[544,128]{1,0:T(8,128)(2,1)S(1)}, u32[]{:S(2)}, u32[]{:S(2)}) collective-permute-start(bf16[544,128]{1,0:T(8,128)(2,1)S(1)} %constant_dynamic-update-slice_fusion.refs_2_), channel_id=1, source_target_pairs={{0,4},{4,0},{8,12},{12,8},{16,20},{20,16},{24,28},{28,24},{1,5},{5... | collective-permute-start | bytes 417800 | tf_op jit(solution)/shard_map/ppermute | solution.py:200

commit v3 on v2

--- a/solution.py
+++ b/solution.py
@@ -20,26 +20,36 @@
 ABT = (((1,), (1,)), ((), ()))
 
 
+def pack_kernel(k_ref, v_ref, place_ref, packet_ref, sems):
+    copies = [
+        pltpu.make_async_copy(ref, packet_ref.at[pl.ds(i * BLOCK, BLOCK)], sems.at[i])
+        for i, ref in enumerate((k_ref, v_ref))
+    ]
+    for copy in copies:
+        copy.start()
+    place = jnp.full((POS_ROWS, HEAD_DIM), place_ref[0], jnp.int32)
+    packet_ref[2 * BLOCK :, :] = place.astype(jnp.float32).astype(packet_ref.dtype)
+    for copy in copies:
+        copy.wait()
+
+
+def in_hbm(array):
+    return pltpu.with_memory_space_constraint(array, pltpu.HBM)
+
+
+HBM_SPEC = pl.BlockSpec(memory_space=pltpu.HBM)
+VMEM_SPEC = pl.BlockSpec(memory_space=pltpu.VMEM)
+
+
 def pack(keys, values, block_position):
-    tag = jnp.broadcast_to(block_position.astype(keys.dtype)[:, None], (POS_ROWS, HEAD_DIM))
-    return jnp.concatenate([keys, values, tag], axis=0)
-
-
-def stage_kernel(source, target, sem):
-    copy = pltpu.make_async_copy(source, target, sem)
-    copy.start()
-    copy.wait()
-
-
-def stage(queries):
     return pl.pallas_call(
-        stage_kernel,
-        out_shape=pltpu.VMEM(queries.shape, queries.dtype),
-        in_specs=[pl.BlockSpec(memory_space=pltpu.HBM)],
-        out_specs=pl.BlockSpec(memory_space=pltpu.VMEM),
-        scratch_shapes=[pltpu.SemaphoreType.DMA],
+        pack_kernel,
+        out_shape=pltpu.VMEM((PACKET, HEAD_DIM), keys.dtype),
+        in_specs=[HBM_SPEC, HBM_SPEC, pl.BlockSpec(memory_space=pltpu.SMEM)],
+        out_specs=VMEM_SPEC,
+        scratch_shapes=[pltpu.SemaphoreType.DMA((2,))],
         compiler_params=pltpu.CompilerParams(vmem_limit_bytes=2**20),
-    )(pltpu.with_memory_space_constraint(queries, pltpu.HBM))
+    )(in_hbm(keys), in_hbm(values), block_position)
 
 
 def attend_kernel(chunk, unroll, first, final, *refs):
@@ -47,7 +57,13 @@
     keys_ref = mine_ref
     if not first:
         keys_ref, old_acc, old_peak, *refs = refs
-    outs, (k_all, vt_all, scores, peaks) = refs[:-4], refs[-4:]
+    *refs, k_all, vt_all, scores, peaks = refs
+    if first:
+        acc_ref, peak_ref, q_here, sems = refs
+    elif final:
+        o_ref, o_here, sems = refs
+    else:
+        acc_ref, peak_ref = refs
     count = keys_ref.shape[0] // PACKET
     total = count * BLOCK
     last = QHEADS // 2 - 1
@@ -55,6 +71,34 @@
     def place(ref, i):
         tag = ref[i * PACKET + 2 * BLOCK : (i + 1) * PACKET, :].astype(jnp.float32)
         return jnp.concatenate([tag[:8], tag[:8]], axis=1)
+
+    own = place(mine_ref, 0)
+    seen = [None if first and i == 0 else place(keys_ref, i) < own for i in range(count)]
+    key = lax.broadcasted_iota(jnp.int32, (BLOCK, PAIR), 0)
+    row = lax.broadcasted_iota(jnp.int32, (BLOCK, PAIR), 1) % BLOCK
+    diagonal = key <= row
+
+    def columns(index, width):
+        if isinstance(index, int):
+            return pl.ds(index * width, width)
+        return pl.ds(pl.multiple_of(index * width, width), width)
+
+    def moved(pair):
+        cols = columns(pair, 2 * HEAD_DIM)
+        source, target = (q_ref, q_here) if first else (o_here, o_ref)
+        return pltpu.make_async_copy(source.at[:, cols], target.at[:, cols], sems.at[pair])
+
+    def pair_queries(pair):
+        source = q_ref
+        if first:
+            moved(pair).wait()
+            source = q_here
+        heads = [source[:, columns(2 * pair + j, HEAD_DIM)] for j in range(2)]
+        return jnp.concatenate(heads, axis=0)
+
+    if first:
+        for pair in range(last + 1):
+            moved(pair).start()
 
     vt_all[HEAD_DIM:, :] = jnp.ones((POS_ROWS, total), vt_all.dtype)
     for i in range(count):
@@ -62,20 +106,6 @@
         rows = slice(i * BLOCK, (i + 1) * BLOCK)
         k_all[rows, :] = keys_ref[base : base + BLOCK, :]
         vt_all[:HEAD_DIM, rows] = keys_ref[base + BLOCK : base + 2 * BLOCK, :].T
-
-    own = place(mine_ref, 0)
-    seen = [None if first and i == 0 else place(keys_ref, i) < own for i in range(count)]
-    key = lax.broadcasted_iota(jnp.int32, (BLOCK, PAIR), 0)
-    row = lax.broadcasted_iota(jnp.int32, (BLOCK, PAIR), 1) % BLOCK
-    diagonal = key <= row
-
-    def columns(head):
-        if isinstance(head, int):
-            return slice(head * HEAD_DIM, (head + 1) * HEAD_DIM)
-        return pl.ds(pl.multiple_of(head * HEAD_DIM, HEAD_DIM), HEAD_DIM)
-
-    def pair_queries(pair):
-        return jnp.concatenate([q_ref[:, columns(2 * pair + j)] for j in range(2)], axis=0)
 
     def score(slot, start, q, peak):
         s = lax.dot_general(
@@ -113,7 +143,7 @@
         if not first:
             peak = jnp.maximum(peak, old_peak[pair])
         if not final:
-            outs[1][pair] = peak
+            peak_ref[pair] = peak
         peaks[slot] = peak
 
     def write(pair, acc, peak):
@@ -122,11 +152,12 @@
             old = old_acc[pair].reshape(-1, 8, PAIR) * alpha[None]
             acc = acc + old.reshape(acc.shape)
         if not final:
-            outs[0][pair] = acc
+            acc_ref[pair] = acc
             return
-        out = (acc[:HEAD_DIM] / acc[HEAD_DIM : HEAD_DIM + 1]).astype(outs[0].dtype)
+        out = (acc[:HEAD_DIM] / acc[HEAD_DIM : HEAD_DIM + 1]).astype(o_here.dtype)
         for j in range(2):
-            outs[0][:, columns(2 * pair + j)] = out[:, j * BLOCK : (j + 1) * BLOCK].T
+            o_here[:, columns(2 * pair + j, HEAD_DIM)] = out[:, j * BLOCK : (j + 1) * BLOCK].T
+        moved(pair).start()
 
     def step(pair, slot, ahead):
         q = pair_queries(pair + 1) if ahead else None
@@ -157,39 +188,53 @@
         lax.fori_loop(0, last // 2, two, 0)
         step(last - 1, 0, True)
     step(last, last % 2, False)
+    if final:
+        for pair in range(last + 1):
+            moved(pair).wait()
 
 
 def attend(queries, mine, state, keys, final):
+    first = state is None
     total = keys.shape[0] // PACKET * BLOCK
     chunk = math.gcd(total, 4 * BLOCK)
-    vmem = pl.BlockSpec(memory_space=pltpu.VMEM)
-    args = (queries, mine) if state is None else (queries, mine, keys, *state)
-    shapes = (
-        jax.ShapeDtypeStruct((QHEADS // 2, HEAD_DIM + POS_ROWS, PAIR), jnp.float32),
-        jax.ShapeDtypeStruct((QHEADS // 2, 8, PAIR), jnp.float32),
-    )
+    pairs = QHEADS // 2
+    args = (in_hbm(queries), mine) if first else (queries, mine, keys, *state)
+    in_specs = [HBM_SPEC if first else VMEM_SPEC] + [VMEM_SPEC] * (len(args) - 1)
+    scratch = [
+        pltpu.VMEM((total, HEAD_DIM), jnp.bfloat16),
+        pltpu.VMEM((HEAD_DIM + POS_ROWS, total), jnp.bfloat16),
+        pltpu.VMEM((2, total, PAIR), jnp.float32),
+        pltpu.VMEM((2, 8, PAIR), jnp.float32),
+    ]
+    if final:
+        shapes = jax.ShapeDtypeStruct(queries.shape, queries.dtype)
+        out_specs = HBM_SPEC
+        scratch = [pltpu.VMEM(queries.shape, queries.dtype), pltpu.SemaphoreType.DMA((pairs,))] + scratch
+    else:
+        shapes = [
+            pltpu.VMEM((pairs, HEAD_DIM + POS_ROWS, PAIR), jnp.float32),
+            pltpu.VMEM((pairs, 8, PAIR), jnp.float32),
+        ]
+        if first:
+            shapes.append(pltpu.VMEM(queries.shape, queries.dtype))
+            scratch = [pltpu.SemaphoreType.DMA((pairs,))] + scratch
+        out_specs = [VMEM_SPEC] * len(shapes)
     return pl.pallas_call(
-        functools.partial(attend_kernel, chunk, total == chunk, state is None, final),
-        out_shape=jax.ShapeDtypeStruct(queries.shape, queries.dtype) if final else shapes,
-        in_specs=[vmem] * len(args),
-        out_specs=vmem if final else (vmem, vmem),
-        scratch_shapes=[
-            pltpu.VMEM((total, HEAD_DIM), jnp.bfloat16),
-            pltpu.VMEM((HEAD_DIM + POS_ROWS, total), jnp.bfloat16),
-            pltpu.VMEM((2, total, PAIR), jnp.float32),
-            pltpu.VMEM((2, 8, PAIR), jnp.float32),
-        ],
+        functools.partial(attend_kernel, chunk, total == chunk, first, final),
+        out_shape=shapes,
+        in_specs=in_specs,
+        out_specs=out_specs,
+        scratch_shapes=scratch,
         compiler_params=pltpu.CompilerParams(vmem_limit_bytes=24 * 2**20),
     )(*args)
 
 
 def body(size, queries, keys, values, block_position):
-    packet = lax.optimization_barrier(pack(keys, values, block_position))
+    packet = pack(keys, values, block_position)
     arrived = []
     for shift in range(size - CORES, 0, -CORES):
         pairs = [(i, (i + shift) % size) for i in range(size)]
         arrived.append(lax.ppermute(packet, "ctx", pairs))
-    queries = stage(queries)
     arrived.append(packet)
     arrived.reverse()
     half = len(arrived) // 2
@@ -199,6 +244,8 @@
         mine = group if mine is None else mine
         partner = lax.ppermute(group, "ctx", [(i, i ^ 1) for i in range(size)])
         state = attend(queries, mine, state, group, False)
+        if name == "near":
+            *state, queries = state
         state = attend(queries, mine, state, partner, name == "far")
     return state
 

time: 19 us -> 19.6 us (1.032)
  Pallas kernels: 6.41 us -> 7.96 us
  other arithmetic: 0.89 us -> 0.01 us
    pallas_call x5, Pallas kernels: 6.41 us -> 7.96 us  [the longest x4 7.17 us: attend(): pl.pallas_call(functools.partial(attend_kernel, chunk, total == chunk, fi...]
    concatenate x1 -> x0, other arithmetic: 0.88 us -> none  [pack(): return jnp.concatenate([keys, values, tag], axis=0)]
  transfers between devices with their start and end apart: 5 -> 5, of which waited for: 3 -> 3; matrix products, arithmetic and copies ran while one was open for 0% -> 0% of each run, Pallas kernels for 24% -> 27%
where the time goes in v3:
time: 19.6 us; the launch traced here: 19.4 us
  Pallas kernels  7.96 us (41%)
  starting transfers between devices  7.18 us (37%)
  waiting for transfers between devices  3.5 us (18%)
  between operations  0.72 us (4%)
    pallas_call x4, Pallas kernels, attend(): pl.pallas_call(functools.partial(attend_kernel, chunk, total == chunk, fi...  7.17 us
    ppermute x3, starting transfers between devices, body(): arrived.append(lax.ppermute(packet, 'ctx', pairs))  7.04 us
    ppermute x3, waiting for transfers between devices, body(): arrived.append(lax.ppermute(packet, 'ctx', pairs))  3.5 us
    pallas_call x1, Pallas kernels, pack(): pl.pallas_call(pack_kernel, out_shape=pltpu.VMEM((PACKET, HEAD_DIM), keys...  0.79 us
  transfers between devices with their start and end apart: 5, of which 3 were waited for; matrix products, arithmetic and copies ran while one was open for 0% of the time, Pallas kernels for 27%

profile of v3, /device:TPU:0, one launch (start us, length us, event | category | flops | bytes accessed | tf_op | source)
XLA Modules:
  0.0 19.4 jit_solution(9103930924250185456)
XLA Ops:
  0.7 0.8 %shard_map.46 = bf16[272,128]{1,0:T(8,128)(2,1)S(1)} custom-call(bf16[128,128]{1,0:T(8,128)(2,1)} %k_ref.1, bf16[128,128]{1,0:T(8,128)(2,1)} %v_ref.1, s32[1]{0:T(128)S(6)} %copy.6.place_ref), custom_call_target="tpu_custom_call" | custom-call | tf_op jit(solution)/shard_map/pallas_call | solution.py:45
  1.5 3.1 %collective-permute-start = (bf16[272,128]{1,0:T(8,128)(2,1)S(1)}, bf16[272,128]{1,0:T(8,128)(2,1)S(1)}, u32[]{:S(2)}, u32[]{:S(2)}) collective-permute-start(bf16[272,128]{1,0:T(8,128)(2,1)S(1)} %shard_map.46), channel_id=1, source_target_pairs={{0,8},{4,12},{8,16},{12,20},{16,24},{20,28},{24,0},{28,4},{1,9},{5... | collective-permute-start | bytes 208904 | tf_op jit(solution)/shard_map/ppermute | solution.py:237
  4.6 2.6 %collective-permute-start.1 = (bf16[272,128]{1,0:T(8,128)(2,1)S(1)}, bf16[272,128]{1,0:T(8,128)(2,1)S(1)}, u32[]{:S(2)}, u32[]{:S(2)}) collective-permute-start(bf16[272,128]{1,0:T(8,128)(2,1)S(1)} %shard_map.46), channel_id=1, source_target_pairs={{0,16},{4,20},{8,24},{12,28},{16,0},{20,4},{24,8},{28,12},{1,17},{... | collective-permute-start | bytes 208904 | tf_op jit(solution)/shard_map/ppermute | solution.py:237
  7.1 1.3 %collective-permute-start.2 = (bf16[272,128]{1,0:T(8,128)(2,1)S(1)}, bf16[272,128]{1,0:T(8,128)(2,1)S(1)}, u32[]{:S(2)}, u32[]{:S(2)}) collective-permute-start(bf16[272,128]{1,0:T(8,128)(2,1)S(1)} %shard_map.46), channel_id=1, source_target_pairs={{0,24},{4,28},{8,0},{12,4},{16,8},{20,12},{24,16},{28,20},{1,25},{... | collective-permute-start | bytes 208904 | tf_op jit(solution)/shard_map/ppermute | solution.py:237
  8.5 0.6 %collective-permute-done = bf16[272,128]{1,0:T(8,128)(2,1)S(1)} collective-permute-done((bf16[272,128]{1,0:T(8,128)(2,1)S(1)}, bf16[272,128]{1,0:T(8,128)(2,1)S(1)}, u32[]{:S(2)}, u32[]{:S(2)}) %collective-permute-start) | collective-permute-done | bytes 69664 | tf_op jit(solution)/shard_map/ppermute | solution.py:237
  9.1 0.1 collective-permute-start.4
  9.2 2.6 %collective-permute-done.1 = bf16[272,128]{1,0:T(8,128)(2,1)S(1)} collective-permute-done((bf16[272,128]{1,0:T(8,128)(2,1)S(1)}, bf16[272,128]{1,0:T(8,128)(2,1)S(1)}, u32[]{:S(2)}, u32[]{:S(2)}) %collective-permute-start.1) | collective-permute-done | bytes 69664 | tf_op jit(solution)/shard_map/ppermute | solution.py:237
  11.9 0.2 %collective-permute-done.2 = bf16[272,128]{1,0:T(8,128)(2,1)S(1)} collective-permute-done((bf16[272,128]{1,0:T(8,128)(2,1)S(1)}, bf16[272,128]{1,0:T(8,128)(2,1)S(1)}, u32[]{:S(2)}, u32[]{:S(2)}) %collective-permute-start.2) | collective-permute-done | bytes 69664 | tf_op jit(solution)/shard_map/ppermute | solution.py:237
  12.1 0.1 collective-permute-start.3
  12.2 3.0 %shard_map.47 = (f32[8,144,256]{2,1,0:T(8,128)S(1)}, f32[8,8,256]{2,1,0:T(8,128)S(1)}, bf16[128,2048]{1,0:T(8,128)(2,1)S(1)}) custom-call(bf16[128,2048]{1,0:T(8,128)(2,1)} %refs_0_.1, bf16[544,128]{1,0:T(8,128)(2,1)S(1)} %pad_maximum_fusion.refs_1_), custom_call_target="tpu_custom_call" | custom-call | tf_op jit(solution)/shard_map/pallas_call | solution.py:222
  15.2 0.0 collective-permute-done.4.refs_2_
  15.2 1.1 %shard_map.48 = (f32[8,144,256]{2,1,0:T(8,128)S(1)}, f32[8,8,256]{2,1,0:T(8,128)S(1)}) custom-call(bf16[128,2048]{1,0:T(8,128)(2,1)S(1)} %get-tuple-element.12.refs_0_, bf16[544,128]{1,0:T(8,128)(2,1)S(1)} %pad_maximum_fusion.refs_1_, bf16[544,128]{1,0:T(8,128)(2,1)S(1)} %collective-permute-done.4.refs_2_, f32[8,144,256]{2,1,0:T(8,128)S(1)} %get-tuple-element.13.refs_3_, ...), custom_call_target="tpu_custom_call" | custom-call | tf_op jit(solution)/shard_map/pallas_call | solution.py:222
  16.4 1.1 %shard_map.49 = (f32[8,144,256]{2,1,0:T(8,128)S(1)}, f32[8,8,256]{2,1,0:T(8,128)S(1)}) custom-call(bf16[128,2048]{1,0:T(8,128)(2,1)S(1)} %get-tuple-element.12.refs_0_, bf16[544,128]{1,0:T(8,128)(2,1)S(1)} %pad_maximum_fusion.refs_1_, bf16[544,128]{1,0:T(8,128)(2,1)S(1)} %constant_dynamic-update-slice_fusion.refs_2_, ...), custom_call_target="tpu_custom_call" | custom-call | tf_op jit(solution)/shard_map/pallas_call | solution.py:222
  17.5 0.0 collective-permute-done.3.refs_2_
  17.5 1.9 %shard_map.50 = bf16[128,2048]{1,0:T(8,128)(2,1)} custom-call(bf16[128,2048]{1,0:T(8,128)(2,1)S(1)} %get-tuple-element.12.refs_0_, bf16[544,128]{1,0:T(8,128)(2,1)S(1)} %pad_maximum_fusion.refs_1_, bf16[544,128]{1,0:T(8,128)(2,1)S(1)} %collective-permute-done.3.refs_2_, f32[8,144,256]{2,1,0:T(8,128)S(1)} %get-tuple-element.17.refs_3_, ...), custom_call_target="tpu_custom_call" | custom-call | tf_op jit(solution)/shard_map/pallas_call | solution.py:222
  (3 shorter events, 0.0 us)
Async XLA Ops:
  1.5 7.7 %collective-permute-start = (bf16[272,128]{1,0:T(8,128)(2,1)S(1)}, bf16[272,128]{1,0:T(8,128)(2,1)S(1)}, u32[]{:S(2)}, u32[]{:S(2)}) collective-permute-start(bf16[272,128]{1,0:T(8,128)(2,1)S(1)} %shard_map.46), channel_id=1, source_target_pairs={{0,8},{4,12},{8,16},{12,20},{16,24},{20,28},{24,0},{28,4},{1,9},{5... | collective-permute-start | bytes 208904 | tf_op jit(solution)/shard_map/ppermute | solution.py:237
  4.6 7.3 %collective-permute-start.1 = (bf16[272,128]{1,0:T(8,128)(2,1)S(1)}, bf16[272,128]{1,0:T(8,128)(2,1)S(1)}, u32[]{:S(2)}, u32[]{:S(2)}) collective-permute-start(bf16[272,128]{1,0:T(8,128)(2,1)S(1)} %shard_map.46), channel_id=1, source_target_pairs={{0,16},{4,20},{8,24},{12,28},{16,0},{20,4},{24,8},{28,12},{1,17},{... | collective-permute-start | bytes 208904 | tf_op jit(solution)/shard_map/ppermute | solution.py:237
  7.1 4.9 %collective-permute-start.2 = (bf16[272,128]{1,0:T(8,128)(2,1)S(1)}, bf16[272,128]{1,0:T(8,128)(2,1)S(1)}, u32[]{:S(2)}, u32[]{:S(2)}) collective-permute-start(bf16[272,128]{1,0:T(8,128)(2,1)S(1)} %shard_map.46), channel_id=1, source_target_pairs={{0,24},{4,28},{8,0},{12,4},{16,8},{20,12},{24,16},{28,20},{1,25},{... | collective-permute-start | bytes 208904 | tf_op jit(solution)/shard_map/ppermute | solution.py:237
  9.1 6.1 %collective-permute-start.4 = (bf16[544,128]{1,0:T(8,128)(2,1)S(1)}, bf16[544,128]{1,0:T(8,128)(2,1)S(1)}, u32[]{:S(2)}, u32[]{:S(2)}) collective-permute-start(bf16[544,128]{1,0:T(8,128)(2,1)S(1)} %pad_maximum_fusion.refs_1_), channel_id=1, source_target_pairs={{0,4},{4,0},{8,12},{12,8},{16,20},{20,16},{24,28},{28,24},{1,5},{5... | collective-permute-start | bytes 417800 | tf_op jit(solution)/shard_map/ppermute | solution.py:245
  12.1 5.4 %collective-permute-start.3 = (bf16[544,128]{1,0:T(8,128)(2,1)S(1)}, bf16[544,128]{1,0:T(8,128)(2,1)S(1)}, u32[]{:S(2)}, u32[]{:S(2)}) collective-permute-start(bf16[544,128]{1,0:T(8,128)(2,1)S(1)} %constant_dynamic-update-slice_fusion.refs_2_), channel_id=1, source_target_pairs={{0,4},{4,0},{8,12},{12,8},{16,20},{20,16},{24,28},{28,24},{1,5},{5... | collective-permute-start | bytes 417800 | tf_op jit(solution)/shard_map/ppermute | solution.py:245

commit v4 on v2

--- a/solution.py
+++ b/solution.py
@@ -15,31 +15,54 @@
 CORES = 2
 POS_ROWS = 16
 PACKET = 2 * BLOCK + POS_ROWS
+PARTS = 2
 PAIR = 2 * BLOCK
 LOG2E_SCALE = math.log2(math.e) / math.sqrt(HEAD_DIM)
 ABT = (((1,), (1,)), ((), ()))
 
 
+def ones_kernel(ones_ref):
+    ones_ref[...] = jnp.ones(ones_ref.shape, ones_ref.dtype)
+
+
+def tag_kernel(place_ref, ones_ref, tag_ref):
+    tag_ref[...] = (ones_ref[...] * place_ref[0].astype(jnp.float32)).astype(tag_ref.dtype)
+
+
+def pack_kernel(k_ref, v_ref, tag_ref, packet_ref):
+    packet_ref[:BLOCK, :] = k_ref[...]
+    packet_ref[BLOCK : 2 * BLOCK, :] = v_ref[...].T
+    packet_ref[2 * BLOCK :, :] = tag_ref[...]
+
+
+VMEM_SPEC = pl.BlockSpec(memory_space=pltpu.VMEM)
+SLOW = pl.CostEstimate(flops=2**40, bytes_accessed=2**14, transcendentals=0)
+SMALL = pltpu.CompilerParams(vmem_limit_bytes=2**20)
+
+
 def pack(keys, values, block_position):
-    tag = jnp.broadcast_to(block_position.astype(keys.dtype)[:, None], (POS_ROWS, HEAD_DIM))
-    return jnp.concatenate([keys, values, tag], axis=0)
-
-
-def stage_kernel(source, target, sem):
-    copy = pltpu.make_async_copy(source, target, sem)
-    copy.start()
-    copy.wait()
-
-
-def stage(queries):
+    ones = pl.pallas_call(
+        ones_kernel,
+        out_shape=pltpu.VMEM((POS_ROWS, HEAD_DIM), jnp.float32),
+        out_specs=VMEM_SPEC,
+        compiler_params=SMALL,
+        cost_estimate=SLOW,
+    )()
+    block_position, ones = lax.optimization_barrier((block_position, ones))
+    tag = pl.pallas_call(
+        tag_kernel,
+        out_shape=pltpu.VMEM((POS_ROWS, HEAD_DIM), keys.dtype),
+        in_specs=[pl.BlockSpec(memory_space=pltpu.SMEM), VMEM_SPEC],
+        out_specs=VMEM_SPEC,
+        compiler_params=SMALL,
+    )(block_position, ones)
     return pl.pallas_call(
-        stage_kernel,
-        out_shape=pltpu.VMEM(queries.shape, queries.dtype),
-        in_specs=[pl.BlockSpec(memory_space=pltpu.HBM)],
-        out_specs=pl.BlockSpec(memory_space=pltpu.VMEM),
-        scratch_shapes=[pltpu.SemaphoreType.DMA],
-        compiler_params=pltpu.CompilerParams(vmem_limit_bytes=2**20),
-    )(pltpu.with_memory_space_constraint(queries, pltpu.HBM))
+        pack_kernel,
+        out_shape=pltpu.VMEM((PACKET, HEAD_DIM), keys.dtype),
+        in_specs=[VMEM_SPEC] * 3,
+        out_specs=VMEM_SPEC,
+        compiler_params=SMALL,
+    )(keys, values, tag)
 
 
 def attend_kernel(chunk, unroll, first, final, *refs):
@@ -48,6 +71,13 @@
     if not first:
         keys_ref, old_acc, old_peak, *refs = refs
     outs, (k_all, vt_all, scores, peaks) = refs[:-4], refs[-4:]
+    if final:
+        o_ref, *outs, sems = outs
+
+        def leave(part):
+            width = o_ref.shape[1] // PARTS
+            cols = pl.ds(part * width, width)
+            return pltpu.make_async_copy(outs[0].at[:, cols], o_ref.at[:, cols], sems.at[part])
     count = keys_ref.shape[0] // PACKET
     total = count * BLOCK
     last = QHEADS // 2 - 1
@@ -61,7 +91,7 @@
         base = i * PACKET
         rows = slice(i * BLOCK, (i + 1) * BLOCK)
         k_all[rows, :] = keys_ref[base : base + BLOCK, :]
-        vt_all[:HEAD_DIM, rows] = keys_ref[base + BLOCK : base + 2 * BLOCK, :].T
+        vt_all[:HEAD_DIM, rows] = keys_ref[base + BLOCK : base + 2 * BLOCK, :]
 
     own = place(mine_ref, 0)
     seen = [None if first and i == 0 else place(keys_ref, i) < own for i in range(count)]
@@ -124,7 +154,9 @@
         if not final:
             outs[0][pair] = acc
             return
-        out = (acc[:HEAD_DIM] / acc[HEAD_DIM : HEAD_DIM + 1]).astype(outs[0].dtype)
+        inverse = 1.0 / acc[HEAD_DIM : HEAD_DIM + 8]
+        out = acc[:HEAD_DIM].reshape(HEAD_DIM // 8, 8, PAIR) * inverse[None]
+        out = out.reshape(HEAD_DIM, PAIR).astype(outs[0].dtype)
         for j in range(2):
             outs[0][:, columns(2 * pair + j)] = out[:, j * BLOCK : (j + 1) * BLOCK].T
 
@@ -147,6 +179,8 @@
     if unroll:
         for pair in range(last):
             step(pair, pair % 2, True)
+            if final and (pair + 1) * PARTS % (last + 1) == 0:
+                leave((pair + 1) * PARTS // (last + 1) - 1).start()
     else:
 
         def two(i, carry):
@@ -156,7 +190,14 @@
 
         lax.fori_loop(0, last // 2, two, 0)
         step(last - 1, 0, True)
+        if final:
+            for part in range(PARTS - 1):
+                leave(part).start()
     step(last, last % 2, False)
+    if final:
+        leave(PARTS - 1).start()
+        for part in range(PARTS):
+            leave(part).wait()
 
 
 def attend(queries, mine, state, keys, final):
@@ -164,6 +205,9 @@
     chunk = math.gcd(total, 4 * BLOCK)
     vmem = pl.BlockSpec(memory_space=pltpu.VMEM)
     args = (queries, mine) if state is None else (queries, mine, keys, *state)
+    leaving = []
+    if final:
+        leaving = [pltpu.VMEM(queries.shape, queries.dtype), pltpu.SemaphoreType.DMA((PARTS,))]
     shapes = (
         jax.ShapeDtypeStruct((QHEADS // 2, HEAD_DIM + POS_ROWS, PAIR), jnp.float32),
         jax.ShapeDtypeStruct((QHEADS // 2, 8, PAIR), jnp.float32),
@@ -172,8 +216,9 @@
         functools.partial(attend_kernel, chunk, total == chunk, state is None, final),
         out_shape=jax.ShapeDtypeStruct(queries.shape, queries.dtype) if final else shapes,
         in_specs=[vmem] * len(args),
-        out_specs=vmem if final else (vmem, vmem),
-        scratch_shapes=[
+        out_specs=pl.BlockSpec(memory_space=pltpu.HBM) if final else (vmem, vmem),
+        scratch_shapes=leaving
+        + [
             pltpu.VMEM((total, HEAD_DIM), jnp.bfloat16),
             pltpu.VMEM((HEAD_DIM + POS_ROWS, total), jnp.bfloat16),
             pltpu.VMEM((2, total, PAIR), jnp.float32),
@@ -184,12 +229,11 @@
 
 
 def body(size, queries, keys, values, block_position):
-    packet = lax.optimization_barrier(pack(keys, values, block_position))
+    packet = pack(keys, values, block_position)
     arrived = []
     for shift in range(size - CORES, 0, -CORES):
         pairs = [(i, (i + shift) % size) for i in range(size)]
         arrived.append(lax.ppermute(packet, "ctx", pairs))
-    queries = stage(queries)
     arrived.append(packet)
     arrived.reverse()
     half = len(arrived) // 2

time: 19 us -> 17.1 us (0.900)
  Pallas kernels: 6.41 us -> 5.39 us
  other arithmetic: 0.89 us -> 0.01 us
    pallas_call x1 -> x3, Pallas kernels: 1.05 us -> 0.07 us  [the longest x1 0.06 us: pack(): pl.pallas_call(pack_kernel, out_shape=pltpu.VMEM((PACKET, HEAD_DIM), keys...]
    concatenate x1 -> x0, other arithmetic: 0.88 us -> none  [pack(): return jnp.concatenate([keys, values, tag], axis=0)]
  transfers between devices with their start and end apart: 5 -> 5, of which waited for: 3 -> 3; matrix products, arithmetic and copies ran while one was open for 0% -> 0% of each run, Pallas kernels for 24% -> 20%
where the time goes in v4:
time: 17.1 us; the launch traced here: 16.9 us
  starting transfers between devices  7.18 us (42%)
  Pallas kernels  5.39 us (32%)
  waiting for transfers between devices  3.5 us (20%)
  between operations  0.79 us (5%)
    ppermute x3, starting transfers between devices, body(): arrived.append(lax.ppermute(packet, 'ctx', pairs))  7.04 us
    pallas_call x4, Pallas kernels, attend(): pl.pallas_call(functools.partial(attend_kernel, chunk, total == chunk, st...  5.32 us
    ppermute x3, waiting for transfers between devices, body(): arrived.append(lax.ppermute(packet, 'ctx', pairs))  3.5 us
  transfers between devices with their start and end apart: 5, of which 3 were waited for; matrix products, arithmetic and copies ran while one was open for 0% of the time, Pallas kernels for 20%

profile of v4, /device:TPU:0, one launch (start us, length us, event | category | flops | bytes accessed | tf_op | source)
XLA Modules:
  0.0 16.9 jit_solution(9289541485538678735)
XLA Ops:
  0.0 0.0 copy-start.1
  0.0 0.0 copy-start.2
  0.0 0.0 copy-start
  0.7 0.0 copy-done.1
  0.8 0.0 copy-done.2
  0.8 0.1 shard_map.48
  0.8 3.1 %collective-permute-start = (bf16[272,128]{1,0:T(8,128)(2,1)S(1)}, bf16[272,128]{1,0:T(8,128)(2,1)S(1)}, u32[]{:S(2)}, u32[]{:S(2)}) collective-permute-start(bf16[272,128]{1,0:T(8,128)(2,1)S(1)} %shard_map.48), channel_id=1, source_target_pairs={{0,8},{4,12},{8,16},{12,20},{16,24},{20,28},{24,0},{28,4},{1,9},{5... | collective-permute-start | bytes 208904 | tf_op jit(solution)/shard_map/ppermute | solution.py:236
  4.0 2.6 %collective-permute-start.1 = (bf16[272,128]{1,0:T(8,128)(2,1)S(1)}, bf16[272,128]{1,0:T(8,128)(2,1)S(1)}, u32[]{:S(2)}, u32[]{:S(2)}) collective-permute-start(bf16[272,128]{1,0:T(8,128)(2,1)S(1)} %shard_map.48), channel_id=1, source_target_pairs={{0,16},{4,20},{8,24},{12,28},{16,0},{20,4},{24,8},{28,12},{1,17},{... | collective-permute-start | bytes 208904 | tf_op jit(solution)/shard_map/ppermute | solution.py:236
  6.5 1.3 %collective-permute-start.2 = (bf16[272,128]{1,0:T(8,128)(2,1)S(1)}, bf16[272,128]{1,0:T(8,128)(2,1)S(1)}, u32[]{:S(2)}, u32[]{:S(2)}) collective-permute-start(bf16[272,128]{1,0:T(8,128)(2,1)S(1)} %shard_map.48), channel_id=1, source_target_pairs={{0,24},{4,28},{8,0},{12,4},{16,8},{20,12},{24,16},{28,20},{1,25},{... | collective-permute-start | bytes 208904 | tf_op jit(solution)/shard_map/ppermute | solution.py:236
  7.9 0.6 %collective-permute-done = bf16[272,128]{1,0:T(8,128)(2,1)S(1)} collective-permute-done((bf16[272,128]{1,0:T(8,128)(2,1)S(1)}, bf16[272,128]{1,0:T(8,128)(2,1)S(1)}, u32[]{:S(2)}, u32[]{:S(2)}) %collective-permute-start) | collective-permute-done | bytes 69664 | tf_op jit(solution)/shard_map/ppermute | solution.py:236
  8.5 0.1 collective-permute-start.4
  8.6 2.6 %collective-permute-done.1 = bf16[272,128]{1,0:T(8,128)(2,1)S(1)} collective-permute-done((bf16[272,128]{1,0:T(8,128)(2,1)S(1)}, bf16[272,128]{1,0:T(8,128)(2,1)S(1)}, u32[]{:S(2)}, u32[]{:S(2)}) %collective-permute-start.1) | collective-permute-done | bytes 69664 | tf_op jit(solution)/shard_map/ppermute | solution.py:236
  11.3 0.2 %collective-permute-done.2 = bf16[272,128]{1,0:T(8,128)(2,1)S(1)} collective-permute-done((bf16[272,128]{1,0:T(8,128)(2,1)S(1)}, bf16[272,128]{1,0:T(8,128)(2,1)S(1)}, u32[]{:S(2)}, u32[]{:S(2)}) %collective-permute-start.2) | collective-permute-done | bytes 69664 | tf_op jit(solution)/shard_map/ppermute | solution.py:236
  11.5 0.1 collective-permute-start.3
  11.6 0.0 copy-done
  11.6 1.1 %shard_map.49 = (f32[8,144,256]{2,1,0:T(8,128)S(1)}, f32[8,8,256]{2,1,0:T(8,128)S(1)}) custom-call(bf16[128,2048]{1,0:T(8,128)(2,1)S(1)} %copy-done, bf16[544,128]{1,0:T(8,128)(2,1)S(1)} %pad_maximum_fusion.refs_1_), custom_call_target="tpu_custom_call" | custom-call | tf_op jit(solution)/shard_map/pallas_call | solution.py:215
  12.7 0.0 collective-permute-done.4.refs_2_
  12.7 1.1 %shard_map.50 = (f32[8,144,256]{2,1,0:T(8,128)S(1)}, f32[8,8,256]{2,1,0:T(8,128)S(1)}) custom-call(bf16[128,2048]{1,0:T(8,128)(2,1)S(1)} %copy-done, bf16[544,128]{1,0:T(8,128)(2,1)S(1)} %pad_maximum_fusion.refs_1_, bf16[544,128]{1,0:T(8,128)(2,1)S(1)} %collective-permute-done.4.refs_2_, f32[8,144,256]{2,1,0:T(8,128)S(1)} %get-tuple-element.15.refs_3_, ...), custom_call_target="tpu_custom_call" | custom-call | tf_op jit(solution)/shard_map/pallas_call | solution.py:215
  13.9 1.1 %shard_map.51 = (f32[8,144,256]{2,1,0:T(8,128)S(1)}, f32[8,8,256]{2,1,0:T(8,128)S(1)}) custom-call(bf16[128,2048]{1,0:T(8,128)(2,1)S(1)} %copy-done, bf16[544,128]{1,0:T(8,128)(2,1)S(1)} %pad_maximum_fusion.refs_1_, bf16[544,128]{1,0:T(8,128)(2,1)S(1)} %constant_dynamic-update-slice_fusion.refs_2_, f32[8,144,256]{2,1,0:T(8,128)S(1)} %get-tuple-element.17.refs_3_, ...), custom_call_target="tpu_custom_call" | custom-call | tf_op jit(solution)/shard_map/pallas_call | solution.py:215
  15.0 0.0 collective-permute-done.3.refs_2_
  15.0 1.9 %shard_map.52 = bf16[128,2048]{1,0:T(8,128)(2,1)} custom-call(bf16[128,2048]{1,0:T(8,128)(2,1)S(1)} %copy-done, bf16[544,128]{1,0:T(8,128)(2,1)S(1)} %pad_maximum_fusion.refs_1_, bf16[544,128]{1,0:T(8,128)(2,1)S(1)} %collective-permute-done.3.refs_2_, f32[8,144,256]{2,1,0:T(8,128)S(1)} %get-tuple-element.19.refs_3_, f32[8,8,256]{2,1,0:T(8,128)S(1)} %get-tuple-element.20.refs_4_), custom_call_target="tpu_custom_call" | custom-call | tf_op jit(solution)/shard_map/pallas_call | solution.py:215
  (5 shorter events, 0.0 us)
Async XLA Ops:
  0.0 0.8 %copy-start.1 = (bf16[128,128]{1,0:T(8,128)(2,1)S(1)}, bf16[128,128]{1,0:T(8,128)(2,1)}, u32[]{:S(2)}) copy-start(bf16[128,128]{1,0:T(8,128)(2,1)} %k_ref.1) | copy-start | bytes 98308
  0.0 0.8 %copy-start.2 = (bf16[128,128]{1,0:T(8,128)(2,1)S(1)}, bf16[128,128]{1,0:T(8,128)(2,1)}, u32[]{:S(2)}) copy-start(bf16[128,128]{1,0:T(8,128)(2,1)} %v_ref.1) | copy-start | bytes 98308
  0.0 11.6 %copy-start = (bf16[128,2048]{1,0:T(8,128)(2,1)S(1)}, bf16[128,2048]{1,0:T(8,128)(2,1)}, u32[]{:S(2)}) copy-start(bf16[128,2048]{1,0:T(8,128)(2,1)} %refs_0_.7) | copy-start | bytes 1572868
  0.8 7.7 %collective-permute-start = (bf16[272,128]{1,0:T(8,128)(2,1)S(1)}, bf16[272,128]{1,0:T(8,128)(2,1)S(1)}, u32[]{:S(2)}, u32[]{:S(2)}) collective-permute-start(bf16[272,128]{1,0:T(8,128)(2,1)S(1)} %shard_map.48), channel_id=1, source_target_pairs={{0,8},{4,12},{8,16},{12,20},{16,24},{20,28},{24,0},{28,4},{1,9},{5... | collective-permute-start | bytes 208904 | tf_op jit(solution)/shard_map/ppermute | solution.py:236
  4.0 7.3 %collective-permute-start.1 = (bf16[272,128]{1,0:T(8,128)(2,1)S(1)}, bf16[272,128]{1,0:T(8,128)(2,1)S(1)}, u32[]{:S(2)}, u32[]{:S(2)}) collective-permute-start(bf16[272,128]{1,0:T(8,128)(2,1)S(1)} %shard_map.48), channel_id=1, source_target_pairs={{0,16},{4,20},{8,24},{12,28},{16,0},{20,4},{24,8},{28,12},{1,17},{... | collective-permute-start | bytes 208904 | tf_op jit(solution)/shard_map/ppermute | solution.py:236
  6.5 4.9 %collective-permute-start.2 = (bf16[272,128]{1,0:T(8,128)(2,1)S(1)}, bf16[272,128]{1,0:T(8,128)(2,1)S(1)}, u32[]{:S(2)}, u32[]{:S(2)}) collective-permute-start(bf16[272,128]{1,0:T(8,128)(2,1)S(1)} %shard_map.48), channel_id=1, source_target_pairs={{0,24},{4,28},{8,0},{12,4},{16,8},{20,12},{24,16},{28,20},{1,25},{... | collective-permute-start | bytes 208904 | tf_op jit(solution)/shard_map/ppermute | solution.py:236
  8.5 4.2 %collective-permute-start.4 = (bf16[544,128]{1,0:T(8,128)(2,1)S(1)}, bf16[544,128]{1,0:T(8,128)(2,1)S(1)}, u32[]{:S(2)}, u32[]{:S(2)}) collective-permute-start(bf16[544,128]{1,0:T(8,128)(2,1)S(1)} %pad_maximum_fusion.refs_1_), channel_id=1, source_target_pairs={{0,4},{4,0},{8,12},{12,8},{16,20},{20,16},{24,28},{28,24},{1,5},{5... | collective-permute-start | bytes 417800 | tf_op jit(solution)/shard_map/ppermute | solution.py:244
  11.5 3.5 %collective-permute-start.3 = (bf16[544,128]{1,0:T(8,128)(2,1)S(1)}, bf16[544,128]{1,0:T(8,128)(2,1)S(1)}, u32[]{:S(2)}, u32[]{:S(2)}) collective-permute-start(bf16[544,128]{1,0:T(8,128)(2,1)S(1)} %constant_dynamic-update-slice_fusion.refs_2_), channel_id=1, source_target_pairs={{0,4},{4,0},{8,12},{12,8},{16,20},{20,16},{24,28},{28,24},{1,5},{5... | collective-permute-start | bytes 417800 | tf_op jit(solution)/shard_map/ppermute | solution.py:244

commit v5 on v4

--- a/solution.py
+++ b/solution.py
@@ -160,26 +160,30 @@
         for j in range(2):
             outs[0][:, columns(2 * pair + j)] = out[:, j * BLOCK : (j + 1) * BLOCK].T
 
+    depth = scores.shape[0] - 1
+
     def step(pair, slot, ahead):
-        q = pair_queries(pair + 1) if ahead else None
+        q = pair_queries(pair + depth) if ahead else None
+        there = (slot + depth) % (depth + 1)
         bound = peaks[slot]
         peak = acc = None
         for start in range(0, total, chunk):
             if ahead:
-                peak = score(1 - slot, start, q, peak)
+                peak = score(there, start, q, peak)
             acc = weigh(slot, start, bound, acc)
         if ahead:
-            keep(pair + 1, 1 - slot, peak)
+            keep(pair + depth, there, peak)
         write(pair, acc, bound)
 
-    q, peak = pair_queries(0), None
-    for start in range(0, total, chunk):
-        peak = score(0, start, q, peak)
-    keep(0, 0, peak)
+    for pair in range(depth):
+        q, peak = pair_queries(pair), None
+        for start in range(0, total, chunk):
+            peak = score(pair, start, q, peak)
+        keep(pair, pair, peak)
     if unroll:
-        for pair in range(last):
-            step(pair, pair % 2, True)
-            if final and (pair + 1) * PARTS % (last + 1) == 0:
+        for pair in range(last + 1):
+            step(pair, pair % (depth + 1), pair + depth <= last)
+            if final and pair < last and (pair + 1) * PARTS % (last + 1) == 0:
                 leave((pair + 1) * PARTS // (last + 1) - 1).start()
     else:
 
@@ -193,7 +197,7 @@
         if final:
             for part in range(PARTS - 1):
                 leave(part).start()
-    step(last, last % 2, False)
+        step(last, last % 2, False)
     if final:
         leave(PARTS - 1).start()
         for part in range(PARTS):
@@ -203,6 +207,7 @@
 def attend(queries, mine, state, keys, final):
     total = keys.shape[0] // PACKET * BLOCK
     chunk = math.gcd(total, 4 * BLOCK)
+    depth = 8 if total == chunk else 1
     vmem = pl.BlockSpec(memory_space=pltpu.VMEM)
     args = (queries, mine) if state is None else (queries, mine, keys, *state)
     leaving = []
@@ -221,8 +226,8 @@
         + [
             pltpu.VMEM((total, HEAD_DIM), jnp.bfloat16),
             pltpu.VMEM((HEAD_DIM + POS_ROWS, total), jnp.bfloat16),
-            pltpu.VMEM((2, total, PAIR), jnp.float32),
-            pltpu.VMEM((2, 8, PAIR), jnp.float32),
+            pltpu.VMEM((depth + 1, total, PAIR), jnp.float32),
+            pltpu.VMEM((depth + 1, 8, PAIR), jnp.float32),
         ],
         compiler_params=pltpu.CompilerParams(vmem_limit_bytes=24 * 2**20),
     )(*args)

time: 17.1 us -> 15.9 us (0.930)
  Pallas kernels: 5.39 us -> 4.22 us
    pallas_call x4, Pallas kernels: 5.32 us -> 4.15 us  [attend(): pl.pallas_call(functools.partial(attend_kernel, chunk, total == chunk, st...]
  transfers between devices with their start and end apart: 5 -> 5, of which waited for: 3 -> 3; matrix products, arithmetic and copies ran while one was open for 0% -> 0% of each run, Pallas kernels for 20% -> 16%
where the time goes in v5:
time: 15.9 us; the launch traced here: 15.8 us
  starting transfers between devices  7.18 us (45%)
  Pallas kernels  4.22 us (27%)
  waiting for transfers between devices  3.5 us (22%)
  between operations  0.79 us (5%)
    ppermute x3, starting transfers between devices, body(): arrived.append(lax.ppermute(packet, 'ctx', pairs))  7.04 us
    pallas_call x4, Pallas kernels, attend(): pl.pallas_call(functools.partial(attend_kernel, chunk, total == chunk, st...  4.15 us
    ppermute x3, waiting for transfers between devices, body(): arrived.append(lax.ppermute(packet, 'ctx', pairs))  3.5 us
  transfers between devices with their start and end apart: 5, of which 3 were waited for; matrix products, arithmetic and copies ran while one was open for 0% of the time, Pallas kernels for 16%

profile of v5, /device:TPU:0, one launch (start us, length us, event | category | flops | bytes accessed | tf_op | source)
XLA Modules:
  0.0 15.8 jit_solution(13855647775961669003)
XLA Ops:
  0.0 0.0 copy-start.1
  0.0 0.0 copy-start.2
  0.0 0.0 copy-start
  0.7 0.0 copy-done.1
  0.8 0.0 copy-done.2
  0.8 0.1 shard_map.48
  0.8 3.1 %collective-permute-start = (bf16[272,128]{1,0:T(8,128)(2,1)S(1)}, bf16[272,128]{1,0:T(8,128)(2,1)S(1)}, u32[]{:S(2)}, u32[]{:S(2)}) collective-permute-start(bf16[272,128]{1,0:T(8,128)(2,1)S(1)} %shard_map.48), channel_id=1, source_target_pairs={{0,8},{4,12},{8,16},{12,20},{16,24},{20,28},{24,0},{28,4},{1,9},{5... | collective-permute-start | bytes 208904 | tf_op jit(solution)/shard_map/ppermute | solution.py:241
  4.0 2.6 %collective-permute-start.1 = (bf16[272,128]{1,0:T(8,128)(2,1)S(1)}, bf16[272,128]{1,0:T(8,128)(2,1)S(1)}, u32[]{:S(2)}, u32[]{:S(2)}) collective-permute-start(bf16[272,128]{1,0:T(8,128)(2,1)S(1)} %shard_map.48), channel_id=1, source_target_pairs={{0,16},{4,20},{8,24},{12,28},{16,0},{20,4},{24,8},{28,12},{1,17},{... | collective-permute-start | bytes 208904 | tf_op jit(solution)/shard_map/ppermute | solution.py:241
  6.5 1.3 %collective-permute-start.2 = (bf16[272,128]{1,0:T(8,128)(2,1)S(1)}, bf16[272,128]{1,0:T(8,128)(2,1)S(1)}, u32[]{:S(2)}, u32[]{:S(2)}) collective-permute-start(bf16[272,128]{1,0:T(8,128)(2,1)S(1)} %shard_map.48), channel_id=1, source_target_pairs={{0,24},{4,28},{8,0},{12,4},{16,8},{20,12},{24,16},{28,20},{1,25},{... | collective-permute-start | bytes 208904 | tf_op jit(solution)/shard_map/ppermute | solution.py:241
  7.9 0.6 %collective-permute-done = bf16[272,128]{1,0:T(8,128)(2,1)S(1)} collective-permute-done((bf16[272,128]{1,0:T(8,128)(2,1)S(1)}, bf16[272,128]{1,0:T(8,128)(2,1)S(1)}, u32[]{:S(2)}, u32[]{:S(2)}) %collective-permute-start) | collective-permute-done | bytes 69664 | tf_op jit(solution)/shard_map/ppermute | solution.py:241
  8.5 0.1 collective-permute-start.4
  8.6 2.6 %collective-permute-done.1 = bf16[272,128]{1,0:T(8,128)(2,1)S(1)} collective-permute-done((bf16[272,128]{1,0:T(8,128)(2,1)S(1)}, bf16[272,128]{1,0:T(8,128)(2,1)S(1)}, u32[]{:S(2)}, u32[]{:S(2)}) %collective-permute-start.1) | collective-permute-done | bytes 69664 | tf_op jit(solution)/shard_map/ppermute | solution.py:241
  11.3 0.2 %collective-permute-done.2 = bf16[272,128]{1,0:T(8,128)(2,1)S(1)} collective-permute-done((bf16[272,128]{1,0:T(8,128)(2,1)S(1)}, bf16[272,128]{1,0:T(8,128)(2,1)S(1)}, u32[]{:S(2)}, u32[]{:S(2)}) %collective-permute-start.2) | collective-permute-done | bytes 69664 | tf_op jit(solution)/shard_map/ppermute | solution.py:241
  11.5 0.1 collective-permute-start.3
  11.6 0.0 copy-done
  11.6 0.8 %shard_map.49 = (f32[8,144,256]{2,1,0:T(8,128)S(1)}, f32[8,8,256]{2,1,0:T(8,128)S(1)}) custom-call(bf16[128,2048]{1,0:T(8,128)(2,1)S(1)} %copy-done, bf16[544,128]{1,0:T(8,128)(2,1)S(1)} %pad_maximum_fusion.refs_1_), custom_call_target="tpu_custom_call" | custom-call | tf_op jit(solution)/shard_map/pallas_call | solution.py:220
  12.4 0.0 collective-permute-done.4.refs_2_
  12.5 0.8 %shard_map.50 = (f32[8,144,256]{2,1,0:T(8,128)S(1)}, f32[8,8,256]{2,1,0:T(8,128)S(1)}) custom-call(bf16[128,2048]{1,0:T(8,128)(2,1)S(1)} %copy-done, bf16[544,128]{1,0:T(8,128)(2,1)S(1)} %pad_maximum_fusion.refs_1_, bf16[544,128]{1,0:T(8,128)(2,1)S(1)} %collective-permute-done.4.refs_2_, f32[8,144,256]{2,1,0:T(8,128)S(1)} %get-tuple-element.15.refs_3_, ...), custom_call_target="tpu_custom_call" | custom-call | tf_op jit(solution)/shard_map/pallas_call | solution.py:220
  13.3 0.8 %shard_map.51 = (f32[8,144,256]{2,1,0:T(8,128)S(1)}, f32[8,8,256]{2,1,0:T(8,128)S(1)}) custom-call(bf16[128,2048]{1,0:T(8,128)(2,1)S(1)} %copy-done, bf16[544,128]{1,0:T(8,128)(2,1)S(1)} %pad_maximum_fusion.refs_1_, bf16[544,128]{1,0:T(8,128)(2,1)S(1)} %constant_dynamic-update-slice_fusion.refs_2_, f32[8,144,256]{2,1,0:T(8,128)S(1)} %get-tuple-element.17.refs_3_, ...), custom_call_target="tpu_custom_call" | custom-call | tf_op jit(solution)/shard_map/pallas_call | solution.py:220
  14.1 0.0 collective-permute-done.3.refs_2_
  14.1 1.6 %shard_map.52 = bf16[128,2048]{1,0:T(8,128)(2,1)} custom-call(bf16[128,2048]{1,0:T(8,128)(2,1)S(1)} %copy-done, bf16[544,128]{1,0:T(8,128)(2,1)S(1)} %pad_maximum_fusion.refs_1_, bf16[544,128]{1,0:T(8,128)(2,1)S(1)} %collective-permute-done.3.refs_2_, f32[8,144,256]{2,1,0:T(8,128)S(1)} %get-tuple-element.19.refs_3_, f32[8,8,256]{2,1,0:T(8,128)S(1)} %get-tuple-element.20.refs_4_), custom_call_target="tpu_custom_call" | custom-call | tf_op jit(solution)/shard_map/pallas_call | solution.py:220
  (5 shorter events, 0.0 us)
Async XLA Ops:
  0.0 0.8 %copy-start.1 = (bf16[128,128]{1,0:T(8,128)(2,1)S(1)}, bf16[128,128]{1,0:T(8,128)(2,1)}, u32[]{:S(2)}) copy-start(bf16[128,128]{1,0:T(8,128)(2,1)} %k_ref.1) | copy-start | bytes 98308
  0.0 0.8 %copy-start.2 = (bf16[128,128]{1,0:T(8,128)(2,1)S(1)}, bf16[128,128]{1,0:T(8,128)(2,1)}, u32[]{:S(2)}) copy-start(bf16[128,128]{1,0:T(8,128)(2,1)} %v_ref.1) | copy-start | bytes 98308
  0.0 11.6 %copy-start = (bf16[128,2048]{1,0:T(8,128)(2,1)S(1)}, bf16[128,2048]{1,0:T(8,128)(2,1)}, u32[]{:S(2)}) copy-start(bf16[128,2048]{1,0:T(8,128)(2,1)} %refs_0_.7) | copy-start | bytes 1572868
  0.8 7.7 %collective-permute-start = (bf16[272,128]{1,0:T(8,128)(2,1)S(1)}, bf16[272,128]{1,0:T(8,128)(2,1)S(1)}, u32[]{:S(2)}, u32[]{:S(2)}) collective-permute-start(bf16[272,128]{1,0:T(8,128)(2,1)S(1)} %shard_map.48), channel_id=1, source_target_pairs={{0,8},{4,12},{8,16},{12,20},{16,24},{20,28},{24,0},{28,4},{1,9},{5... | collective-permute-start | bytes 208904 | tf_op jit(solution)/shard_map/ppermute | solution.py:241
  4.0 7.3 %collective-permute-start.1 = (bf16[272,128]{1,0:T(8,128)(2,1)S(1)}, bf16[272,128]{1,0:T(8,128)(2,1)S(1)}, u32[]{:S(2)}, u32[]{:S(2)}) collective-permute-start(bf16[272,128]{1,0:T(8,128)(2,1)S(1)} %shard_map.48), channel_id=1, source_target_pairs={{0,16},{4,20},{8,24},{12,28},{16,0},{20,4},{24,8},{28,12},{1,17},{... | collective-permute-start | bytes 208904 | tf_op jit(solution)/shard_map/ppermute | solution.py:241
  6.5 4.9 %collective-permute-start.2 = (bf16[272,128]{1,0:T(8,128)(2,1)S(1)}, bf16[272,128]{1,0:T(8,128)(2,1)S(1)}, u32[]{:S(2)}, u32[]{:S(2)}) collective-permute-start(bf16[272,128]{1,0:T(8,128)(2,1)S(1)} %shard_map.48), channel_id=1, source_target_pairs={{0,24},{4,28},{8,0},{12,4},{16,8},{20,12},{24,16},{28,20},{1,25},{... | collective-permute-start | bytes 208904 | tf_op jit(solution)/shard_map/ppermute | solution.py:241
  8.5 3.9 %collective-permute-start.4 = (bf16[544,128]{1,0:T(8,128)(2,1)S(1)}, bf16[544,128]{1,0:T(8,128)(2,1)S(1)}, u32[]{:S(2)}, u32[]{:S(2)}) collective-permute-start(bf16[544,128]{1,0:T(8,128)(2,1)S(1)} %pad_maximum_fusion.refs_1_), channel_id=1, source_target_pairs={{0,4},{4,0},{8,12},{12,8},{16,20},{20,16},{24,28},{28,24},{1,5},{5... | collective-permute-start | bytes 417800 | tf_op jit(solution)/shard_map/ppermute | solution.py:249
  11.5 2.6 %collective-permute-start.3 = (bf16[544,128]{1,0:T(8,128)(2,1)S(1)}, bf16[544,128]{1,0:T(8,128)(2,1)S(1)}, u32[]{:S(2)}, u32[]{:S(2)}) collective-permute-start(bf16[544,128]{1,0:T(8,128)(2,1)S(1)} %constant_dynamic-update-slice_fusion.refs_2_), channel_id=1, source_target_pairs={{0,4},{4,0},{8,12},{12,8},{16,20},{20,16},{24,28},{28,24},{1,5},{5... | collective-permute-start | bytes 417800 | tf_op jit(solution)/shard_map/ppermute | solution.py:249

commit v6 on v5

--- a/solution.py
+++ b/solution.py
@@ -13,9 +13,10 @@
 QHEADS = 16
 BLOCK = 128
 CORES = 2
-POS_ROWS = 16
-PACKET = 2 * BLOCK + POS_ROWS
-PARTS = 2
+ONES_ROWS = 16
+TAG_ROWS = 8
+PACKET = 2 * BLOCK + TAG_ROWS
+PARTS = 4
 PAIR = 2 * BLOCK
 LOG2E_SCALE = math.log2(math.e) / math.sqrt(HEAD_DIM)
 ABT = (((1,), (1,)), ((), ()))
@@ -43,7 +44,7 @@
 def pack(keys, values, block_position):
     ones = pl.pallas_call(
         ones_kernel,
-        out_shape=pltpu.VMEM((POS_ROWS, HEAD_DIM), jnp.float32),
+        out_shape=pltpu.VMEM((TAG_ROWS, HEAD_DIM), jnp.float32),
         out_specs=VMEM_SPEC,
         compiler_params=SMALL,
         cost_estimate=SLOW,
@@ -51,7 +52,7 @@
     block_position, ones = lax.optimization_barrier((block_position, ones))
     tag = pl.pallas_call(
         tag_kernel,
-        out_shape=pltpu.VMEM((POS_ROWS, HEAD_DIM), keys.dtype),
+        out_shape=pltpu.VMEM((TAG_ROWS, HEAD_DIM), keys.dtype),
         in_specs=[pl.BlockSpec(memory_space=pltpu.SMEM), VMEM_SPEC],
         out_specs=VMEM_SPEC,
         compiler_params=SMALL,
@@ -86,7 +87,7 @@
         tag = ref[i * PACKET + 2 * BLOCK : (i + 1) * PACKET, :].astype(jnp.float32)
         return jnp.concatenate([tag[:8], tag[:8]], axis=1)
 
-    vt_all[HEAD_DIM:, :] = jnp.ones((POS_ROWS, total), vt_all.dtype)
+    vt_all[HEAD_DIM:, :] = jnp.ones((ONES_ROWS, total), vt_all.dtype)
     for i in range(count):
         base = i * PACKET
         rows = slice(i * BLOCK, (i + 1) * BLOCK)
@@ -214,7 +215,7 @@
     if final:
         leaving = [pltpu.VMEM(queries.shape, queries.dtype), pltpu.SemaphoreType.DMA((PARTS,))]
     shapes = (
-        jax.ShapeDtypeStruct((QHEADS // 2, HEAD_DIM + POS_ROWS, PAIR), jnp.float32),
+        jax.ShapeDtypeStruct((QHEADS // 2, HEAD_DIM + ONES_ROWS, PAIR), jnp.float32),
         jax.ShapeDtypeStruct((QHEADS // 2, 8, PAIR), jnp.float32),
     )
     return pl.pallas_call(
@@ -225,7 +226,7 @@
         scratch_shapes=leaving
         + [
             pltpu.VMEM((total, HEAD_DIM), jnp.bfloat16),
-            pltpu.VMEM((HEAD_DIM + POS_ROWS, total), jnp.bfloat16),
+            pltpu.VMEM((HEAD_DIM + ONES_ROWS, total), jnp.bfloat16),
             pltpu.VMEM((depth + 1, total, PAIR), jnp.float32),
             pltpu.VMEM((depth + 1, 8, PAIR), jnp.float32),
         ],

time: 15.9 us -> 15.8 us (level)
  waiting for transfers between devices: 3.5 us -> 3.34 us
    ppermute x3, waiting for transfers between devices: 3.5 us -> 3.33 us  [body(): arrived.append(lax.ppermute(packet, 'ctx', pairs))]
where the time goes in v6:
time: 15.8 us; the launch traced here: 15.6 us
  starting transfers between devices  7.18 us (45%)
  Pallas kernels  4.24 us (27%)
  waiting for transfers between devices  3.34 us (21%)
  between operations  0.78 us (5%)
    ppermute x3, starting transfers between devices, body(): arrived.append(lax.ppermute(packet, 'ctx', pairs))  7.04 us
    pallas_call x4, Pallas kernels, attend(): pl.pallas_call(functools.partial(attend_kernel, chunk, total == chunk, st...  4.17 us
    ppermute x3, waiting for transfers between devices, body(): arrived.append(lax.ppermute(packet, 'ctx', pairs))  3.33 us
  transfers between devices with their start and end apart: 5, of which 3 were waited for; matrix products, arithmetic and copies ran while one was open for 0% of the time, Pallas kernels for 16%

profile of v6, /device:TPU:0, one launch (start us, length us, event | category | flops | bytes accessed | tf_op | source)
XLA Modules:
  0.0 15.6 jit_solution(5396608533180218193)
XLA Ops:
  0.0 0.0 copy-start.1
  0.0 0.0 copy-start.2
  0.0 0.0 copy-start
  0.7 0.0 copy-done.1
  0.8 0.0 copy-done.2
  0.8 0.1 shard_map.48
  0.8 3.1 %collective-permute-start = (bf16[264,128]{1,0:T(8,128)(2,1)S(1)}, bf16[264,128]{1,0:T(8,128)(2,1)S(1)}, u32[]{:S(2)}, u32[]{:S(2)}) collective-permute-start(bf16[264,128]{1,0:T(8,128)(2,1)S(1)} %shard_map.48), channel_id=1, source_target_pairs={{0,8},{4,12},{8,16},{12,20},{16,24},{20,28},{24,0},{28,4},{1,9},{5... | collective-permute-start | bytes 202760 | tf_op jit(solution)/shard_map/ppermute | solution.py:242
  4.0 2.6 %collective-permute-start.1 = (bf16[264,128]{1,0:T(8,128)(2,1)S(1)}, bf16[264,128]{1,0:T(8,128)(2,1)S(1)}, u32[]{:S(2)}, u32[]{:S(2)}) collective-permute-start(bf16[264,128]{1,0:T(8,128)(2,1)S(1)} %shard_map.48), channel_id=1, source_target_pairs={{0,16},{4,20},{8,24},{12,28},{16,0},{20,4},{24,8},{28,12},{1,17},{... | collective-permute-start | bytes 202760 | tf_op jit(solution)/shard_map/ppermute | solution.py:242
  6.5 1.3 %collective-permute-start.2 = (bf16[264,128]{1,0:T(8,128)(2,1)S(1)}, bf16[264,128]{1,0:T(8,128)(2,1)S(1)}, u32[]{:S(2)}, u32[]{:S(2)}) collective-permute-start(bf16[264,128]{1,0:T(8,128)(2,1)S(1)} %shard_map.48), channel_id=1, source_target_pairs={{0,24},{4,28},{8,0},{12,4},{16,8},{20,12},{24,16},{28,20},{1,25},{... | collective-permute-start | bytes 202760 | tf_op jit(solution)/shard_map/ppermute | solution.py:242
  7.9 0.6 %collective-permute-done = bf16[264,128]{1,0:T(8,128)(2,1)S(1)} collective-permute-done((bf16[264,128]{1,0:T(8,128)(2,1)S(1)}, bf16[264,128]{1,0:T(8,128)(2,1)S(1)}, u32[]{:S(2)}, u32[]{:S(2)}) %collective-permute-start) | collective-permute-done | bytes 67616 | tf_op jit(solution)/shard_map/ppermute | solution.py:242
  8.5 0.1 collective-permute-start.4
  8.6 2.6 %collective-permute-done.1 = bf16[264,128]{1,0:T(8,128)(2,1)S(1)} collective-permute-done((bf16[264,128]{1,0:T(8,128)(2,1)S(1)}, bf16[264,128]{1,0:T(8,128)(2,1)S(1)}, u32[]{:S(2)}, u32[]{:S(2)}) %collective-permute-start.1) | collective-permute-done | bytes 67616 | tf_op jit(solution)/shard_map/ppermute | solution.py:242
  11.1 0.2 %collective-permute-done.2 = bf16[264,128]{1,0:T(8,128)(2,1)S(1)} collective-permute-done((bf16[264,128]{1,0:T(8,128)(2,1)S(1)}, bf16[264,128]{1,0:T(8,128)(2,1)S(1)}, u32[]{:S(2)}, u32[]{:S(2)}) %collective-permute-start.2) | collective-permute-done | bytes 67616 | tf_op jit(solution)/shard_map/ppermute | solution.py:242
  11.3 0.1 collective-permute-start.3
  11.4 0.0 copy-done
  11.4 0.9 %shard_map.49 = (f32[8,144,256]{2,1,0:T(8,128)S(1)}, f32[8,8,256]{2,1,0:T(8,128)S(1)}) custom-call(bf16[128,2048]{1,0:T(8,128)(2,1)S(1)} %copy-done, bf16[528,128]{1,0:T(8,128)(2,1)S(1)} %pad_maximum_fusion.refs_1_), custom_call_target="tpu_custom_call" | custom-call | tf_op jit(solution)/shard_map/pallas_call | solution.py:221
  12.3 0.0 collective-permute-done.4.refs_2_
  12.3 0.8 %shard_map.50 = (f32[8,144,256]{2,1,0:T(8,128)S(1)}, f32[8,8,256]{2,1,0:T(8,128)S(1)}) custom-call(bf16[128,2048]{1,0:T(8,128)(2,1)S(1)} %copy-done, bf16[528,128]{1,0:T(8,128)(2,1)S(1)} %pad_maximum_fusion.refs_1_, bf16[528,128]{1,0:T(8,128)(2,1)S(1)} %collective-permute-done.4.refs_2_, f32[8,144,256]{2,1,0:T(8,128)S(1)} %get-tuple-element.15.refs_3_, ...), custom_call_target="tpu_custom_call" | custom-call | tf_op jit(solution)/shard_map/pallas_call | solution.py:221
  13.1 0.8 %shard_map.51 = (f32[8,144,256]{2,1,0:T(8,128)S(1)}, f32[8,8,256]{2,1,0:T(8,128)S(1)}) custom-call(bf16[128,2048]{1,0:T(8,128)(2,1)S(1)} %copy-done, bf16[528,128]{1,0:T(8,128)(2,1)S(1)} %pad_maximum_fusion.refs_1_, bf16[528,128]{1,0:T(8,128)(2,1)S(1)} %constant_dynamic-update-slice_fusion.refs_2_, f32[8,144,256]{2,1,0:T(8,128)S(1)} %get-tuple-element.17.refs_3_, ...), custom_call_target="tpu_custom_call" | custom-call | tf_op jit(solution)/shard_map/pallas_call | solution.py:221
  14.0 0.0 collective-permute-done.3.refs_2_
  14.0 1.6 %shard_map.52 = bf16[128,2048]{1,0:T(8,128)(2,1)} custom-call(bf16[128,2048]{1,0:T(8,128)(2,1)S(1)} %copy-done, bf16[528,128]{1,0:T(8,128)(2,1)S(1)} %pad_maximum_fusion.refs_1_, bf16[528,128]{1,0:T(8,128)(2,1)S(1)} %collective-permute-done.3.refs_2_, f32[8,144,256]{2,1,0:T(8,128)S(1)} %get-tuple-element.19.refs_3_, f32[8,8,256]{2,1,0:T(8,128)S(1)} %get-tuple-element.20.refs_4_), custom_call_target="tpu_custom_call" | custom-call | tf_op jit(solution)/shard_map/pallas_call | solution.py:221
  (5 shorter events, 0.0 us)
Async XLA Ops:
  0.0 0.8 %copy-start.1 = (bf16[128,128]{1,0:T(8,128)(2,1)S(1)}, bf16[128,128]{1,0:T(8,128)(2,1)}, u32[]{:S(2)}) copy-start(bf16[128,128]{1,0:T(8,128)(2,1)} %k_ref.1) | copy-start | bytes 98308
  0.0 0.8 %copy-start.2 = (bf16[128,128]{1,0:T(8,128)(2,1)S(1)}, bf16[128,128]{1,0:T(8,128)(2,1)}, u32[]{:S(2)}) copy-start(bf16[128,128]{1,0:T(8,128)(2,1)} %v_ref.1) | copy-start | bytes 98308
  0.0 11.4 %copy-start = (bf16[128,2048]{1,0:T(8,128)(2,1)S(1)}, bf16[128,2048]{1,0:T(8,128)(2,1)}, u32[]{:S(2)}) copy-start(bf16[128,2048]{1,0:T(8,128)(2,1)} %refs_0_.7) | copy-start | bytes 1572868
  0.8 7.6 %collective-permute-start = (bf16[264,128]{1,0:T(8,128)(2,1)S(1)}, bf16[264,128]{1,0:T(8,128)(2,1)S(1)}, u32[]{:S(2)}, u32[]{:S(2)}) collective-permute-start(bf16[264,128]{1,0:T(8,128)(2,1)S(1)} %shard_map.48), channel_id=1, source_target_pairs={{0,8},{4,12},{8,16},{12,20},{16,24},{20,28},{24,0},{28,4},{1,9},{5... | collective-permute-start | bytes 202760 | tf_op jit(solution)/shard_map/ppermute | solution.py:242
  4.0 7.2 %collective-permute-start.1 = (bf16[264,128]{1,0:T(8,128)(2,1)S(1)}, bf16[264,128]{1,0:T(8,128)(2,1)S(1)}, u32[]{:S(2)}, u32[]{:S(2)}) collective-permute-start(bf16[264,128]{1,0:T(8,128)(2,1)S(1)} %shard_map.48), channel_id=1, source_target_pairs={{0,16},{4,20},{8,24},{12,28},{16,0},{20,4},{24,8},{28,12},{1,17},{... | collective-permute-start | bytes 202760 | tf_op jit(solution)/shard_map/ppermute | solution.py:242
  6.5 4.8 %collective-permute-start.2 = (bf16[264,128]{1,0:T(8,128)(2,1)S(1)}, bf16[264,128]{1,0:T(8,128)(2,1)S(1)}, u32[]{:S(2)}, u32[]{:S(2)}) collective-permute-start(bf16[264,128]{1,0:T(8,128)(2,1)S(1)} %shard_map.48), channel_id=1, source_target_pairs={{0,24},{4,28},{8,0},{12,4},{16,8},{20,12},{24,16},{28,20},{1,25},{... | collective-permute-start | bytes 202760 | tf_op jit(solution)/shard_map/ppermute | solution.py:242
  8.5 3.8 %collective-permute-start.4 = (bf16[528,128]{1,0:T(8,128)(2,1)S(1)}, bf16[528,128]{1,0:T(8,128)(2,1)S(1)}, u32[]{:S(2)}, u32[]{:S(2)}) collective-permute-start(bf16[528,128]{1,0:T(8,128)(2,1)S(1)} %pad_maximum_fusion.refs_1_), channel_id=1, source_target_pairs={{0,4},{4,0},{8,12},{12,8},{16,20},{20,16},{24,28},{28,24},{1,5},{5... | collective-permute-start | bytes 405512 | tf_op jit(solution)/shard_map/ppermute | solution.py:250
  11.3 2.6 %collective-permute-start.3 = (bf16[528,128]{1,0:T(8,128)(2,1)S(1)}, bf16[528,128]{1,0:T(8,128)(2,1)S(1)}, u32[]{:S(2)}, u32[]{:S(2)}) collective-permute-start(bf16[528,128]{1,0:T(8,128)(2,1)S(1)} %constant_dynamic-update-slice_fusion.refs_2_), channel_id=1, source_target_pairs={{0,4},{4,0},{8,12},{12,8},{16,20},{20,16},{24,28},{28,24},{1,5},{5... | collective-permute-start | bytes 405512 | tf_op jit(solution)/shard_map/ppermute | solution.py:250
